TPU v7x, 128 devices: a whole 4x4x4 slice. The times are simulated.
128 devices in a mesh: gx: 8 (over y_lo, z), gy: 16 (over x, y_hi, core).
Axes of the slice: x: 4, y: 4 (y_hi: 2, y_lo: 2; y = y_hi * 2 + y_lo), z: 4, core: 2. Of those that a mesh axis runs over, the one named last changes fastest.
Arguments:
- group_one: bfloat16 [24576, 768], P(('gx', 'gy')), may hold values from -6 to 6
- routes_one: int32 [24576, 1], P(('gx', 'gy')), may hold values from 0 to 127; in each aligned block of 192 rows (0 to 191, 192 to 383, ...) at most 6 rows name the same one
- gates_one: float32 [24576], P(('gx', 'gy')), may hold values from 0.2 to 1
- group_two: bfloat16 [24576, 768], P(('gx', 'gy')), may hold values from -6 to 6
- routes_two: int32 [24576, 1], P(('gx', 'gy')), may hold values from 0 to 127; in each aligned block of 192 rows (0 to 191, 192 to 383, ...) at most 6 rows name the same one
- gates_two: float32 [24576], P(('gx', 'gy')), may hold values from 0.2 to 1
- norm_gain: float32 [768], replicated, may hold values from 0.1 to 1.9
- weight_in: bfloat16 [128, 768, 3072], P(('gx', 'gy')), may hold values from -0.21875 to 0.21875
- weight_out: bfloat16 [128, 3072, 768], P(('gx', 'gy')), may hold values from -0.109375 to 0.109375
- old_place: int32 [128], replicated, may hold values from 0 to 127, each once
- partner: int32 [128], replicated, may hold values from 0 to 127, as said below
Outputs:
- result_one: bfloat16 [24576, 768], P(('gx', 'gy'))
- result_two: bfloat16 [24576, 768], P(('gx', 'gy'))
- new_in: bfloat16 [128, 768, 3072], P(('gx', 'gy'))
- new_out: bfloat16 [128, 3072, 768], P(('gx', 'gy'))
Inputs may be any that keep to these rules, and one draw needn't show every extreme that they name: `routes_one`: at most 6 tokens of one device's rows in a block name the same expert, a bound that some block reaches of some device's rows in every draw. `routes_two`: same law as routes_one. partner is an involution: partner[partner[s]] = s; exactly 64 slots have partner[s] != s.
All inputs are finite; a program needn't handle non-finite values.
Results may differ from a plain program's by a relative error of at most 0.0041.
Values may be sent and summed in bfloat16 or wider, within the bound.
No kernel may reach another device: no remote copies, remote signals or barrier semaphores. Data moves between devices by JAX's collectives and lax.ppermute only.
A program may use at most 128 MiB of HBM per device.

v0:
```python
import jax
import jax.numpy as jnp
from jax import lax
from jax.sharding import PartitionSpec as P

CAP = 6


epsilon = 1e-06


def slot_tables(old_place, partner):
    slot_count = old_place.shape[0]
    labels = lax.iota(jnp.int32, slot_count)
    where_old = jnp.zeros((slot_count,), jnp.int32).at[old_place].set(labels)
    new_place = jnp.take(old_place, partner, axis=0)
    where_new = jnp.zeros((slot_count,), jnp.int32).at[new_place].set(labels)
    return (where_old, where_new)


def expert_pass(arrived, weight_in, weight_out):
    widths = arrived.shape
    inputs = arrived.reshape(-1, widths[2])
    hidden = jnp.maximum(
        jnp.dot(inputs, weight_in[0], preferred_element_type=jnp.float32), 0.0
    ).astype(jnp.bfloat16)
    result = (
        jnp.dot(hidden, weight_out[0], preferred_element_type=jnp.float32)
        .astype(jnp.bfloat16)
        .reshape(widths)
    )
    return lax.all_to_all(result, ("gx", "gy"), split_axis=0, concat_axis=0, tiled=True)


def switch_layer(tokens_in, routes, gate_probs, norm_gain, holder, weight_in, weight_out):
    devices = lax.axis_size(("gx", "gy"))
    model_width = tokens_in.shape[1]
    values = tokens_in.astype(jnp.float32)
    scaling = lax.rsqrt(jnp.mean(values * values, axis=1, keepdims=True) + epsilon)
    normed = (values * scaling * norm_gain).astype(jnp.bfloat16)
    target = jnp.take(holder, routes[:, 0], axis=0)
    member = (target[:, None] == lax.iota(jnp.int32, devices)[None, :]).astype(jnp.int32)
    before = jnp.sum(jnp.cumsum(member, axis=0) * member, axis=1) - 1
    position = target * CAP + before
    outgoing = jnp.zeros((devices * CAP, model_width), jnp.bfloat16).at[position].set(normed)
    outgoing = outgoing.reshape(devices, CAP, model_width)
    returned = (lambda arrived: expert_pass(arrived, weight_in, weight_out))(
        lax.all_to_all(outgoing, ("gx", "gy"), split_axis=0, concat_axis=0, tiled=True)
    )
    answer = jnp.take(returned.reshape(devices * CAP, model_width), position, axis=0).astype(
        jnp.float32
    )
    return (values + gate_probs[:, None] * answer).astype(jnp.bfloat16)


def relocate(weight_in, weight_out, partner):
    devices = lax.axis_size(("gx", "gy"))
    shape_in = weight_in.shape
    shape_out = weight_out.shape
    stacked = jnp.stack([weight_in.reshape(devices, -1), weight_out.reshape(devices, -1)], axis=1)
    pieces = lax.all_to_all(stacked, ("gx", "gy"), split_axis=0, concat_axis=0, tiled=True)
    reordered = jnp.take(pieces, partner, axis=0)
    settled = lax.all_to_all(reordered, ("gx", "gy"), split_axis=0, concat_axis=0, tiled=True)
    return (settled[:, 0].reshape(shape_in), settled[:, 1].reshape(shape_out))


def local(
    group_one,
    routes_one,
    gates_one,
    group_two,
    routes_two,
    gates_two,
    norm_gain,
    weight_in,
    weight_out,
    old_place,
    partner,
):
    where_old, where_new = slot_tables(old_place, partner)
    first_out = switch_layer(
        group_one, routes_one, gates_one, norm_gain, where_old, weight_in, weight_out
    )
    second = switch_layer(
        group_two, routes_two, gates_two, norm_gain, where_old, weight_in, weight_out
    )
    new_in, new_out = relocate(weight_in, weight_out, partner)
    return (first_out, second, new_in, new_out)


def solution(mesh):
    placed = (
        P(("gx", "gy"), None),
        P(("gx", "gy"), None),
        P(("gx", "gy")),
        P(("gx", "gy"), None),
        P(("gx", "gy"), None),
        P(("gx", "gy")),
        P(),
        P(("gx", "gy"), None, None),
        P(("gx", "gy"), None, None),
        P(),
        P(),
    )
    return jax.shard_map(
        local,
        mesh=mesh,
        in_specs=placed,
        out_specs=(
            P(("gx", "gy"), None),
            P(("gx", "gy"), None),
            P(("gx", "gy"), None, None),
            P(("gx", "gy"), None, None),
        ),
        check_vma=False,
    )
```

profile of v0, /device:TPU:37, one launch (start us, length us, event | category | flops | bytes accessed | tf_op | source)
XLA Modules:
  0.0 501.3 jit_solution(17405065527622887866)
XLA Ops:
  3.0 1.6 gather_fusion.3
  6.9 2.2 scatter_custom_fusion.2
  10.5 10.5 %all-to-all-start.2 = ((bf16[128,6,768]{2,1,0:T(8,128)(2,1)}), bf16[128,6,768]{2,1,0:T(8,128)(2,1)S(1)}, u32[]{:S(2)}, u32[]{:S(2)}) async-start(bf16[128,6,768]{2,1,0:T(8,128)(2,1)} %reshape.98), calls=%async_computation.2 | async-start | bytes 3145728 | tf_op jit(solution)/shard_map/all_to_all | solution.py:48
  23.3 1.8 scatter_custom_fusion.1
  26.5 19.8 %stack_reshape.8 = bf16[128,1,18432]{2,1,0:T(2,128)(2,1)} reshape(bf16[1,768,3072]{2,1,0:T(8,128)(2,1)} %param.22) | data formatting | bytes 9437184 | tf_op jit(solution)/shard_map/stack;reshape | solution.py:60
  46.4 19.2 %stack_reshape.9 = bf16[128,1,18432]{2,1,0:T(2,128)(2,1)} reshape(bf16[1,3072,768]{2,1,0:T(8,128)(2,1)} %param.23) | data formatting | bytes 9437184 | tf_op jit(solution)/shard_map/stack;reshape | solution.py:60
  65.6 9.8 %all-to-all-start = ((bf16[128,6,768]{2,1,0:T(8,128)(2,1)}), bf16[128,6,768]{2,1,0:T(8,128)(2,1)S(1)}, u32[]{:S(2)}, u32[]{:S(2)}) async-start(bf16[128,6,768]{2,1,0:T(8,128)(2,1)} %reshape.92), calls=%async_computation | async-start | bytes 3145728 | tf_op jit(solution)/shard_map/all_to_all | solution.py:48
  75.4 22.2 %pad_maximum_fusion = bf16[128,2,18432]{2,1,0:T(2,128)(2,1)} fusion(bf16[128,1,18432]{2,1,0:T(2,128)(2,1)} %stack_reshape.9, bf16[128,1,18432]{2,1,0:T(2,128)(2,1)} %stack_reshape.8), kind=kLoop, calls=%fused_computation.11 | loop fusion | flops 18874368 | bytes 18874368 | tf_op jit(solution)/shard_map/stack | solution.py:60
  97.5 10.2 %all-to-all-start.4 = ((bf16[128,2,18432]{2,1,0:T(2,128)(2,1)}), bf16[128,2,18432]{2,1,0:T(2,128)(2,1)}, u32[]{:S(2)}, u32[]{:S(2)}) async-start(bf16[128,2,18432]{2,1,0:T(2,128)(2,1)} %pad_maximum_fusion), calls=%async_computation.4 | async-start | bytes 18874368 | tf_op jit(solution)/shard_map/all_to_all | solution.py:61
  109.0 11.7 %fusion.9 = bf16[768,768]{1,0:T(8,128)(2,1)S(1)} fusion(bf16[1,3072,768]{2,1,0:T(8,128)(2,1)} %param.23, bf16[768,768]{1,0:T(8,128)(2,1)} %reshape.99, bf16[1,768,3072]{2,1,0:T(8,128)(2,1)} %param.22), kind=kOutput, calls=%fused_computation.21 | convolution fusion | flops 7253065728 | bytes 11796480 | tf_op jit(solution)/shard_map/dot_general | solution.py:28
  122.5 103.9 %all-to-all-done.4 = bf16[128,2,18432]{2,1,0:T(2,128)(2,1)} async-done(((bf16[128,2,18432]{2,1,0:T(2,128)(2,1)}), bf16[128,2,18432]{2,1,0:T(2,128)(2,1)}, u32[]{:S(2)}, u32[]{:S(2)}) %all-to-all-start.4) | async-done | bytes 9437216 | tf_op jit(solution)/shard_map/all_to_all | solution.py:61
  226.4 11.9 %all-to-all-start.3 = ((bf16[128,6,768]{2,1,0:T(8,128)(2,1)}), bf16[128,6,768]{2,1,0:T(8,128)(2,1)S(1)}, u32[]{:S(2)}, u32[]{:S(2)}) async-start(bf16[128,6,768]{2,1,0:T(8,128)(2,1)} %reshape.100), calls=%async_computation.3 | async-start | bytes 3145728 | tf_op jit(solution)/shard_map/all_to_all | solution.py:32
  238.3 12.4 %fusion.6 = bf16[768,768]{1,0:T(8,128)(2,1)} fusion(bf16[1,3072,768]{2,1,0:T(8,128)(2,1)} %param.23, bf16[768,768]{1,0:T(8,128)(2,1)S(1)} %reshape.93, bf16[1,768,3072]{2,1,0:T(8,128)(2,1)} %param.22), kind=kOutput, calls=%fused_computation.20 | convolution fusion | flops 7253065728 | bytes 11796480 | tf_op jit(solution)/shard_map/dot_general | solution.py:28
  250.7 3.2 reshape.94
  253.9 25.7 %gather_fusion = bf16[128,2,18432]{2,1,0:T(2,128)(2,1)} fusion(bf16[128,2,18432]{2,1,0:T(2,128)(2,1)} %all-to-all-done.4, s32[1024]{0:T(1024)S(1)} %pad_clamp_fusion), kind=kCustom, calls=%fused_computation.4 | custom fusion | bytes 18874880 | tf_op jit(solution)/shard_map/jit(_take)/gather | solution.py:62
  279.6 10.2 %all-to-all-start.1 = ((bf16[128,6,768]{2,1,0:T(8,128)(2,1)}), bf16[128,6,768]{2,1,0:T(8,128)(2,1)}, u32[]{:S(2)}, u32[]{:S(2)}) async-start(bf16[128,6,768]{2,1,0:T(8,128)(2,1)} %reshape.94), calls=%async_computation.1 | async-start | bytes 3145728 | tf_op jit(solution)/shard_map/all_to_all | solution.py:32
  289.8 14.3 %broadcast_select_fusion = bf16[128,2,18432]{2,1,0:T(2,128)(2,1)} fusion(bf16[128,2,18432]{2,1,0:T(2,128)(2,1)} %gather_fusion, pred[128]{0:T(512)(128)(4,1)S(1)} %compare_and_fusion.2), kind=kLoop, calls=%fused_computation.8 | loop fusion | flops 4718592 | bytes 18874496 | tf_op jit(solution)/shard_map/jit(_take)/select_n | solution.py:62
  304.1 7.1 %all-to-all-done.1 = bf16[128,6,768]{2,1,0:T(8,128)(2,1)} async-done(((bf16[128,6,768]{2,1,0:T(8,128)(2,1)}), bf16[128,6,768]{2,1,0:T(8,128)(2,1)}, u32[]{:S(2)}, u32[]{:S(2)}) %all-to-all-start.1) | async-done | bytes 1179680 | tf_op jit(solution)/shard_map/all_to_all | solution.py:32
  311.2 7.7 %all-to-all-start.5 = ((bf16[128,2,18432]{2,1,0:T(2,128)(2,1)}), bf16[128,2,18432]{2,1,0:T(2,128)(2,1)}, u32[]{:S(2)}, u32[]{:S(2)}) async-start(bf16[128,2,18432]{2,1,0:T(2,128)(2,1)} %broadcast_select_fusion), calls=%async_computation.5 | async-start | bytes 18874368 | tf_op jit(solution)/shard_map/all_to_all | solution.py:63
  320.4 2.3 reshape.95
  325.7 111.9 %all-to-all-done.5 = bf16[128,2,18432]{2,1,0:T(2,128)(2,1)} async-done(((bf16[128,2,18432]{2,1,0:T(2,128)(2,1)}), bf16[128,2,18432]{2,1,0:T(2,128)(2,1)}, u32[]{:S(2)}, u32[]{:S(2)}) %all-to-all-start.5) | async-done | bytes 9437216 | tf_op jit(solution)/shard_map/all_to_all | solution.py:63
  437.6 46.7 %slice_reduce_fusion = (bf16[128,18432]{1,0:T(8,128)(2,1)}, bf16[128,18432]{1,0:T(8,128)(2,1)}) fusion(bf16[128,2,18432]{2,1,0:T(2,128)(2,1)} %all-to-all-done.5), kind=kLoop, calls=%fused_computation.9 | loop fusion | bytes 18874368 | tf_op jit(solution)/shard_map/slice | solution.py:64
  484.2 9.3 %reshape_squeeze.6 = bf16[1,768,3072]{2,1,0:T(8,128)(2,1)} reshape(bf16[128,18432]{1,0:T(8,128)(2,1)} %get-tuple-element.7) | data formatting | bytes 9437184 | tf_op jit(solution)/shard_map/reshape;squeeze | solution.py:64
  493.6 7.7 %reshape_squeeze.7 = bf16[1,3072,768]{2,1,0:T(8,128)(2,1)} reshape(bf16[128,18432]{1,0:T(8,128)(2,1)} %get-tuple-element.6) | data formatting | bytes 9437184 | tf_op jit(solution)/shard_map/reshape;squeeze | solution.py:64
  (68 shorter events, 17.0 us)
Async XLA Ops:
  3.0 18.0 %copy-start.3 = (s32[192,1]{0,1:T(1,128)S(1)}, s32[192,1]{0,1:T(1,128)}, u32[]{:S(2)}) copy-start(s32[192,1]{0,1:T(1,128)} %param.16) | copy-start | bytes 2308
  6.9 16.3 %copy-start.1 = (bf16[192,768]{1,0:T(8,128)(2,1)S(1)}, bf16[192,768]{1,0:T(8,128)(2,1)}, u32[]{:S(2)}) copy-start(bf16[192,768]{1,0:T(8,128)(2,1)} %param.15) | copy-start | bytes 884740
  6.9 16.4 %copy-start.2 = (f32[768]{0:T(1024)S(1)}, f32[768]{0:T(1024)}, u32[]{:S(2)}) copy-start(f32[768]{0:T(1024)} %param.21) | copy-start | bytes 9220
  10.5 55.1 %all-to-all-start.2 = ((bf16[128,6,768]{2,1,0:T(8,128)(2,1)}), bf16[128,6,768]{2,1,0:T(8,128)(2,1)S(1)}, u32[]{:S(2)}, u32[]{:S(2)}) async-start(bf16[128,6,768]{2,1,0:T(8,128)(2,1)} %reshape.98), calls=%async_computation.2 | async-start | bytes 3145728 | tf_op jit(solution)/shard_map/all_to_all | solution.py:48
  65.6 31.9 %all-to-all-start = ((bf16[128,6,768]{2,1,0:T(8,128)(2,1)}), bf16[128,6,768]{2,1,0:T(8,128)(2,1)S(1)}, u32[]{:S(2)}, u32[]{:S(2)}) async-start(bf16[128,6,768]{2,1,0:T(8,128)(2,1)} %reshape.92), calls=%async_computation | async-start | bytes 3145728 | tf_op jit(solution)/shard_map/all_to_all | solution.py:48
  97.5 10.2 %copy-start.6 = (s32[128]{0:T(128)S(1)}, s32[128]{0:T(128)}, u32[]{:S(2)}) copy-start(s32[128]{0:T(128)} %param.25) | copy-start | bytes 1540
  97.5 128.9 %all-to-all-start.4 = ((bf16[128,2,18432]{2,1,0:T(2,128)(2,1)}), bf16[128,2,18432]{2,1,0:T(2,128)(2,1)}, u32[]{:S(2)}, u32[]{:S(2)}) async-start(bf16[128,2,18432]{2,1,0:T(2,128)(2,1)} %pad_maximum_fusion), calls=%async_computation.4 | async-start | bytes 18874368 | tf_op jit(solution)/shard_map/all_to_all | solution.py:61
  226.4 53.2 %all-to-all-start.3 = ((bf16[128,6,768]{2,1,0:T(8,128)(2,1)}), bf16[128,6,768]{2,1,0:T(8,128)(2,1)S(1)}, u32[]{:S(2)}, u32[]{:S(2)}) async-start(bf16[128,6,768]{2,1,0:T(8,128)(2,1)} %reshape.100), calls=%async_computation.3 | async-start | bytes 3145728 | tf_op jit(solution)/shard_map/all_to_all | solution.py:32
  279.6 31.5 %all-to-all-start.1 = ((bf16[128,6,768]{2,1,0:T(8,128)(2,1)}), bf16[128,6,768]{2,1,0:T(8,128)(2,1)}, u32[]{:S(2)}, u32[]{:S(2)}) async-start(bf16[128,6,768]{2,1,0:T(8,128)(2,1)} %reshape.94), calls=%async_computation.1 | async-start | bytes 3145728 | tf_op jit(solution)/shard_map/all_to_all | solution.py:32
  311.2 126.4 %all-to-all-start.5 = ((bf16[128,2,18432]{2,1,0:T(2,128)(2,1)}), bf16[128,2,18432]{2,1,0:T(2,128)(2,1)}, u32[]{:S(2)}, u32[]{:S(2)}) async-start(bf16[128,2,18432]{2,1,0:T(2,128)(2,1)} %broadcast_select_fusion), calls=%async_computation.5 | async-start | bytes 18874368 | tf_op jit(solution)/shard_map/all_to_all | solution.py:63
  319.4 4.4 copy-start
  319.4 4.4 copy-start.4
  319.4 5.4 %copy-start.5 = (f32[192]{0:T(256)S(1)}, f32[192]{0:T(256)}, u32[]{:S(2)}) copy-start(f32[192]{0:T(256)} %param.17) | copy-start | bytes 2308
where the time goes:
time: 506 us; the launch traced here: 501 us
  waiting for transfers between devices  223 us (44%)
  local copies, waits for them, and re-layouts  146 us (29%)
  starting transfers between devices  60.2 us (12%)
  other arithmetic  46.7 us (9%)
  matrix products  24.1 us (5%)
    all_to_all x1, waiting for transfers between devices, relocate(): lax.all_to_all(reordered, ('gx', 'gy'), split_axis=0, concat_axis=0, tile...  112 us
    all_to_all x1, waiting for transfers between devices, relocate(): lax.all_to_all(stacked, ('gx', 'gy'), split_axis=0, concat_axis=0, tiled=...  104 us
    slice x1, local copies, waits for them, and re-layouts, relocate(): return (settled[:, 0].reshape(shape_in), settled[:, 1].reshape(shape_out))  46.7 us
    another operation x2, local copies, waits for them, and re-layouts, relocate(): jnp.stack([weight_in.reshape(devices, -1), weight_out.reshape(devices, -1...  39.1 us
    gather x1, local copies, waits for them, and re-layouts, relocate(): reordered = jnp.take(pieces, partner, axis=0)  25.7 us
    dot_general x2, matrix products, expert_pass(): jnp.dot(hidden, weight_out[0], preferred_element_type=jnp.float32)  24.1 us
    another operation x1, other arithmetic, relocate(): jnp.stack([weight_in.reshape(devices, -1), weight_out.reshape(devices, -1...  22.2 us
    all_to_all x2, starting transfers between devices, expert_pass(): lax.all_to_all(result, ('gx', 'gy'), split_axis=0, concat_axis=0, tiled=T...  22 us
  transfers between devices with their start and end apart: 6, of which 3 were waited for; matrix products, arithmetic and copies ran while one was open for 29% of the time, Pallas kernels for 0%

commit v1 on v0

v1 whole, which is shorter than its diff:
```python
import functools

import jax
import jax.numpy as jnp
from jax import lax
from jax.experimental import pallas as pl
from jax.experimental.pallas import tpu as pltpu
from jax.sharding import PartitionSpec as P

AXES = ("gx", "gy")
EPS = 1e-06
CAP = 6
N = 128
HALF = 2304
CHUNK = 72
TOK = 9
C1, C2, C3 = 21, 20, 21
NPART = 41
MA2 = 10
MB2 = C2 - MA2

HBM = pl.BlockSpec(memory_space=pltpu.MemorySpace.HBM)
SMEM = pl.BlockSpec(memory_space=pltpu.SMEM)
VMEM = pl.BlockSpec(memory_space=pltpu.VMEM)
BF = jnp.bfloat16


def tiles_of(w, rows, cols):
    return w.reshape(rows // 8, 8, cols // 128, 128).transpose(0, 2, 1, 3).reshape(HALF, 8, 128)


def array_of(t, rows, cols):
    return t.reshape(rows // 8, cols // 128, 8, 128).transpose(0, 2, 1, 3).reshape(1, rows, cols)


def copies(partner, visit):
    def step(j, counts):
        movers, stayers = counts
        p = partner[j]
        moving = p != j
        visit(j, moving, jnp.where(moving, movers, stayers), p)
        one = moving.astype(jnp.int32)
        return (movers + one, stayers + 1 - one)

    lax.fori_loop(0, N, step, (jnp.int32(0), jnp.int32(0)))


def own_piece(w_in, w_out, rank, offset, size, act):
    @pl.when(rank < 32)
    def _():
        act(w_in.at[pl.ds(rank * CHUNK + offset, size)])

    @pl.when(rank >= 32)
    def _():
        act(w_out.at[pl.ds((rank - 32) * CHUNK + offset, size)])


def go(src, dst, sem, wait):
    copy = pltpu.make_async_copy(src, dst, sem)
    if wait:
        copy.wait()
    else:
        copy.start()


def first_kernel(
    me, partner, w_in, w_out, one, two, routes_one, routes_two, gain, place,
    buf1, pos, tok, sem, tsem,
):
    my = me[0]
    i_move = partner[my] != my

    def sends(wait):
        def visit(j, moving, rank, p):
            offset = jnp.where(moving, NPART, 0)
            own_piece(
                w_in, w_out, rank, offset, C1,
                lambda src: go(src, buf1.at[j, pl.ds(0, C1)], sem, wait),
            )

        @pl.when(i_move)
        def _():
            copies(partner, visit)

    sends(False)
    rows = one.shape[0]
    width = one.shape[1]
    total = 2 * rows
    slots = place[...]
    lower = (
        lax.broadcasted_iota(jnp.int32, (rows, rows), 1)
        < lax.broadcasted_iota(jnp.int32, (rows, rows), 0)
    ).astype(jnp.float32).astype(BF)
    lane = lax.broadcasted_iota(jnp.int32, (rows, N), 1)
    normed, target, place_in = [], [], []
    for b, (group, routes) in enumerate(((one, routes_one), (two, routes_two))):
        values = group[...].astype(jnp.float32)
        scaling = lax.rsqrt(jnp.mean(values * values, axis=1, keepdims=True) + EPS)
        normed.append((values * scaling * gain[...]).astype(BF))
        member = routes[...] == slots
        flag = member.astype(jnp.float32)
        before = jnp.dot(lower, flag.astype(BF), preferred_element_type=jnp.float32)
        target.append(jnp.sum(jnp.where(member, lane, 0), axis=1, keepdims=True))
        place_in.append(
            jnp.sum(flag * before, axis=1, keepdims=True).astype(jnp.int32) + b * CAP
        )
    normed = jnp.concatenate(normed, axis=0)
    target = jnp.concatenate(target, axis=0)
    place_in = jnp.concatenate(place_in, axis=0)
    early = jnp.where(place_in < 8, target * 8 + place_in, -1)
    late = jnp.where(place_in < 8, -1, target * 8 + place_in - 8)
    pos[:, 0:1] = early
    pos[:, 1:2] = late
    eye = lax.broadcasted_iota(jnp.int32, (total, total), 0) == lax.broadcasted_iota(
        jnp.int32, (total, total), 1
    )
    early_row = jnp.sum(jnp.where(eye, early, 0), axis=0, keepdims=True)
    late_row = jnp.sum(jnp.where(eye, late, 0), axis=0, keepdims=True)
    row = lax.broadcasted_iota(jnp.int32, (N * 8, total), 0)
    pick = (row == early_row).astype(jnp.float32).astype(BF)
    top = jnp.dot(pick, normed, preferred_element_type=jnp.float32)
    fours = row - (row & 4)
    pick = (fours == late_row).astype(jnp.float32).astype(BF)
    rest = jnp.dot(pick, normed, preferred_element_type=jnp.float32)
    upper = lax.broadcasted_iota(jnp.int32, (N, 8, 128), 1) < 4
    cut = lambda x, c: x[:, c * 128 : (c + 1) * 128].reshape(N, 8, 128)
    for c in range(width // 128):
        tok[:, c] = cut(top, c).astype(BF)
    for c in range(width // 256):
        tok[:, width // 128 + c] = jnp.where(upper, cut(rest, 2 * c), cut(rest, 2 * c + 1)).astype(BF)
    go(tok, buf1.at[:, pl.ds(C1, TOK)], tsem, False)
    go(tok, buf1.at[:, pl.ds(C1, TOK)], tsem, True)
    sends(True)


def second_own_kernel(me, partner, w_in, w_out, buf2, sem):
    my = me[0]

    def sends(wait):
        def visit(j, moving, rank, p):
            @pl.when(moving)
            def _():
                own_piece(
                    w_in, w_out, rank, NPART + C1, MA2,
                    lambda src: go(src, buf2.at[j, pl.ds(0, MA2)], sem, wait),
                )

            @pl.when(jnp.logical_not(moving))
            def _():
                own_piece(
                    w_in, w_out, rank, C1, C2,
                    lambda src: go(src, buf2.at[j, pl.ds(0, C2)], sem, wait),
                )

        @pl.when(partner[my] != my)
        def _():
            copies(partner, visit)

    sends(False)
    sends(True)


def forward_kernel(of_mover, of_stayer, extra, me, partner, recv, *refs):
    if extra:
        tok, _, buf, sem, tsem = refs
        go(tok, buf.at[:, pl.ds(C3, TOK)], tsem, False)
    else:
        *_, buf, sem = refs
    my = me[0]
    i_move = partner[my] != my

    def sends(wait):
        for mine, (lo, to, size) in ((True, of_mover), (False, of_stayer)):
            def visit(j, moving, rank, p):
                @pl.when(moving)
                def _():
                    go(recv.at[p, pl.ds(lo, size)], buf.at[j, pl.ds(to, size)], sem, wait)

            @pl.when(i_move == mine)
            def _():
                copies(partner, visit)

    sends(False)
    sends(True)
    if extra:
        go(tok, buf.at[:, pl.ds(C3, TOK)], tsem, True)


def settle(partner, recv, new_in, new_out, sem, wait, of_mover, of_stayer):
    def visit(j, moving, rank, p):
        for kind, (lo, to, size) in ((True, of_mover), (False, of_stayer)):
            @pl.when(moving == kind)
            def _():
                own_piece(
                    new_in, new_out, rank, to, size,
                    lambda dst: go(recv.at[j, pl.ds(lo, size)], dst, sem, wait),
                )

    copies(partner, visit)


def third_settle_kernel(me, partner, w_in, w_out, recv2, new_in, new_out, sem):
    my = me[0]
    i_move = partner[my] != my

    def sends(wait):
        @pl.when(i_move)
        def _():
            settle(
                partner, recv2, new_in, new_out, sem, wait,
                (MA2, NPART, MB2), (0, 0, C2),
            )

        @pl.when(jnp.logical_not(i_move))
        def _():
            go(w_in, new_in, sem, wait)
            go(w_out, new_out, sem, wait)

    sends(False)
    sends(True)


def last_kernel(
    me, partner, recv3, pos, one, two, gate_one, gate_two, in_, out_,
    res_one, res_two, new_in, new_out, tok, sem, tsem,
):
    my = me[0]
    i_move = partner[my] != my

    go(recv3.at[:, pl.ds(C3, TOK)], tok, tsem, False)

    def sends(wait):
        @pl.when(i_move)
        def _():
            settle(
                partner, recv3, new_in, new_out, sem, wait,
                (0, NPART + MB2, C3), (0, C2, C3),
            )

    sends(False)
    go(recv3.at[:, pl.ds(C3, TOK)], tok, tsem, True)
    rows = one.shape[0]
    width = one.shape[1]
    total = 2 * rows
    early = pos[:, 0:1]
    late = pos[:, 1:2]
    lane = lax.broadcasted_iota(jnp.int32, (total, N * 8), 1)
    hot = lambda where: (lane == where).astype(jnp.float32).astype(BF)
    flat = lambda c: tok[:, c].astype(jnp.float32).reshape(N * 8, 128).astype(BF)
    full = jnp.concatenate([flat(c) for c in range(width // 128)], axis=1)
    tail = jnp.concatenate([flat(width // 128 + c) for c in range(width // 256)], axis=1)
    top = jnp.dot(hot(early), full, preferred_element_type=jnp.float32)
    even = jnp.dot(hot(late), tail, preferred_element_type=jnp.float32)
    odd = jnp.dot(
        hot(jnp.where(late < 0, -1, late + 4)), tail, preferred_element_type=jnp.float32
    )
    for b, (group, gate, res) in enumerate(
        ((one, gate_one, res_one), (two, gate_two, res_two))
    ):
        r = slice(b * rows, (b + 1) * rows)
        for c in range(width // 128):
            s = slice(c * 128, (c + 1) * 128)
            h = slice(c // 2 * 128, (c // 2 + 1) * 128)
            answer = top[r, s] + (odd if c % 2 else even)[r, h]
            res[:, s] = (group[:, s].astype(jnp.float32) + gate[...] * answer).astype(BF)
    sends(True)


def shape(*dims, dtype=BF):
    return jax.ShapeDtypeStruct(dims, dtype)


def exchange(x):
    return lax.all_to_all(x, AXES, split_axis=0, concat_axis=0, tiled=True)


DMA = pltpu.SemaphoreType.DMA(())


def local(
    group_one, routes_one, gates_one, group_two, routes_two, gates_two,
    norm_gain, weight_in, weight_out, old_place, partner,
):
    rows, width = group_one.shape
    ff = weight_in.shape[2]
    me = lax.axis_index(AXES).astype(jnp.int32).reshape(1)
    w_in = tiles_of(weight_in, width, ff)
    w_out = tiles_of(weight_out, ff, width)
    buf1, pos = pl.pallas_call(
        first_kernel,
        out_shape=(shape(N, C1 + TOK, 8, 128), shape(2 * rows, 2, dtype=jnp.int32)),
        in_specs=[SMEM, SMEM, HBM, HBM] + [VMEM] * 6,
        out_specs=(HBM, VMEM),
        scratch_shapes=[pltpu.VMEM((N, TOK, 8, 128), BF), DMA, DMA],
        name="first",
    )(
        me, partner, w_in, w_out, group_one, group_two, routes_one, routes_two,
        norm_gain.reshape(1, width), old_place.reshape(1, N),
    )
    recv1 = exchange(buf1)
    buf2 = pl.pallas_call(
        second_own_kernel,
        out_shape=shape(N, C2, 8, 128),
        in_specs=[SMEM, SMEM, HBM, HBM],
        out_specs=HBM,
        scratch_shapes=[DMA],
        name="second_own",
    )(me, partner, w_in, w_out)
    buf2 = pl.pallas_call(
        functools.partial(forward_kernel, (0, MA2, MB2), (0, 0, C2), False),
        out_shape=shape(N, C2, 8, 128),
        in_specs=[SMEM, SMEM, HBM, HBM],
        out_specs=HBM,
        scratch_shapes=[DMA],
        input_output_aliases={3: 0},
        name="second_forward",
    )(me, partner, recv1, buf2)
    recv2 = exchange(buf2)
    arrived = recv1[:, C1:]
    cols = width // 128
    top = arrived[:, :cols].transpose(0, 2, 1, 3).reshape(N * 8, width)
    rest = arrived[:, cols:].reshape(N, cols // 2, 2, 4, 128)
    rest = rest.transpose(0, 3, 1, 2, 4).reshape(N * 4, width)
    inputs = jnp.concatenate([top, rest], axis=0)
    hidden = jnp.maximum(
        jnp.dot(inputs, weight_in[0], preferred_element_type=jnp.float32), 0.0
    ).astype(BF)
    result = jnp.dot(hidden, weight_out[0], preferred_element_type=jnp.float32).astype(BF)
    top = result[: N * 8].reshape(N, 8, cols, 128).transpose(0, 2, 1, 3)
    rest = result[N * 8 :].reshape(N, 4, cols // 2, 2, 128)
    rest = rest.transpose(0, 2, 3, 1, 4).reshape(N, cols // 2, 8, 128)
    answers = jnp.concatenate([top, rest], axis=1)
    buf3 = pl.pallas_call(
        functools.partial(
            forward_kernel, (MB2, 0, C1 - MB2), (C2, 0, C1 - C2), False
        ),
        out_shape=shape(N, C3 + TOK, 8, 128),
        in_specs=[SMEM, SMEM, HBM],
        out_specs=HBM,
        scratch_shapes=[DMA],
        name="third_held",
    )(me, partner, recv1)
    buf3 = pl.pallas_call(
        functools.partial(
            forward_kernel, (0, C1 - MB2, MA2), (0, C1 - C2, C2), True
        ),
        out_shape=shape(N, C3 + TOK, 8, 128),
        in_specs=[SMEM, SMEM, HBM, pl.BlockSpec(memory_space=pl.ANY), HBM],
        out_specs=HBM,
        scratch_shapes=[DMA, DMA],
        input_output_aliases={4: 0},
        name="third_forward",
    )(me, partner, recv2, answers, buf3)
    recv3 = exchange(buf3)
    new_in, new_out = pl.pallas_call(
        third_settle_kernel,
        out_shape=(shape(HALF, 8, 128), shape(HALF, 8, 128)),
        in_specs=[SMEM, SMEM, HBM, HBM, HBM],
        out_specs=(HBM, HBM),
        scratch_shapes=[DMA],
        name="settle",
    )(me, partner, w_in, w_out, recv2)
    res_one, res_two, new_in, new_out = pl.pallas_call(
        last_kernel,
        out_shape=(
            shape(rows, width), shape(rows, width), shape(HALF, 8, 128), shape(HALF, 8, 128),
        ),
        in_specs=[SMEM, SMEM, HBM] + [VMEM] * 5 + [HBM, HBM],
        out_specs=(VMEM, VMEM, HBM, HBM),
        scratch_shapes=[pltpu.VMEM((N, TOK, 8, 128), BF), DMA, DMA],
        input_output_aliases={8: 2, 9: 3},
        name="last",
    )(
        me, partner, recv3, pos, group_one, group_two,
        gates_one.reshape(rows, 1), gates_two.reshape(rows, 1), new_in, new_out,
    )
    return (res_one, res_two, array_of(new_in, width, ff), array_of(new_out, ff, width))


def solution(mesh):
    split = P(AXES, None)
    flat = P(AXES)
    deep = P(AXES, None, None)
    return jax.shard_map(
        local,
        mesh=mesh,
        in_specs=(split, split, flat, split, split, flat, P(), deep, deep, P(), P()),
        out_specs=(split, split, deep, deep),
        check_vma=False,
    )
```

time: 506 us -> 898 us (1.77)
  Pallas kernels: 0 us -> 539 us
  local copies, waits for them, and re-layouts: 146 us -> 13.6 us
  starting transfers between devices: 60.2 us -> 190 us
  waiting for transfers between devices: 223 us -> 131 us
  other arithmetic: 46.7 us -> 1.6 us
    pallas_call x0 -> x7, Pallas kernels: none -> 539 us  [the longest x1 288 us: local(): pl.pallas_call(third_settle_kernel, out_shape=(shape(HALF, 8, 128), shape...]
    all_to_all x6 -> x3, starting transfers between devices: 60.2 us -> 190 us  [exchange(): return lax.all_to_all(x, AXES, split_axis=0, concat_axis=0, tiled=True)]
    all_to_all x6 -> x3, waiting for transfers between devices: 223 us -> 131 us  [exchange(): return lax.all_to_all(x, AXES, split_axis=0, concat_axis=0, tiled=True)]
    another operation x10 -> x0, local copies, waits for them, and re-layouts: 56.2 us -> none  [the longest x2 39.1 us: relocate(): jnp.stack([weight_in.reshape(devices, -1), weight_out.reshape(devices, -1...]
    slice x1 -> x2, local copies, waits for them, and re-layouts: 46.7 us -> 1.29 us  [the longest x1 1.23 us: local(): rest = arrived[:, cols:].reshape(N, cols // 2, 2, 4, 128)]
    gather x5 -> x0, local copies, waits for them, and re-layouts: 30.9 us -> none  [the longest x1 25.7 us: relocate(): reordered = jnp.take(pieces, partner, axis=0)]
    another operation x9 -> x0, other arithmetic: 22.6 us -> none  [the longest x1 22.2 us: relocate(): jnp.stack([weight_in.reshape(devices, -1), weight_out.reshape(devices, -1...]
    select_n x7 -> x0, other arithmetic: 16.3 us -> none  [the longest x2 14.3 us: relocate(): reordered = jnp.take(pieces, partner, axis=0)]
  transfers between devices with their start and end apart: 6 -> 3, of which waited for: 3 -> 2; matrix products, arithmetic and copies ran while one was open for 29% -> 3% of each run, Pallas kernels for 0% -> 33%
where the time goes in v1:
time: 898 us; the launch traced here: 896 us
  Pallas kernels  539 us (60%)
  starting transfers between devices  190 us (21%)
  waiting for transfers between devices  131 us (15%)
  matrix products  19.7 us (2%)
  local copies, waits for them, and re-layouts  13.6 us (2%)
    pallas_call x1, Pallas kernels, local(): pl.pallas_call(third_settle_kernel, out_shape=(shape(HALF, 8, 128), shape...  288 us
    all_to_all x3, starting transfers between devices, exchange(): return lax.all_to_all(x, AXES, split_axis=0, concat_axis=0, tiled=True)  190 us
    pallas_call x1, Pallas kernels, local(): pl.pallas_call(functools.partial(forward_kernel, (0, C1 - MB2, MA2), (0,...  153 us
    all_to_all x3, waiting for transfers between devices, exchange(): return lax.all_to_all(x, AXES, split_axis=0, concat_axis=0, tiled=True)  131 us
    pallas_call x1, Pallas kernels, local(): pl.pallas_call(functools.partial(forward_kernel, (0, MA2, MB2), (0, 0, C2...  81.3 us
    dot_general x1, matrix products, local(): jnp.dot(hidden, weight_out[0], preferred_element_type=jnp.float32)  19.7 us
  transfers between devices with their start and end apart: 3, of which 2 were waited for; matrix products, arithmetic and copies ran while one was open for 3% of the time, Pallas kernels for 33%

profile of v1, /device:TPU:37, one launch (start us, length us, event | category | flops | bytes accessed | tf_op | source)
XLA Modules:
  0.0 895.9 jit_solution(6051229071264721857)
XLA Ops:
  0.6 1.3 reshape.70.gain
  1.9 1.4 copy.22.routes_one
  3.3 1.4 copy.23.routes_two
  4.8 5.6 first.1
  10.4 174.6 %all-to-all-start = ((bf16[128,30,8,128]{3,2,1,0:T(8,128)(2,1)}), bf16[128,30,8,128]{3,2,1,0:T(8,128)(2,1)}, u32[]{:S(2)}, u32[]{:S(2)}) async-start(bf16[128,30,8,128]{3,2,1,0:T(8,128)(2,1)} %get-tuple-element.12), calls=%async_computation | async-start | bytes 15728640 | tf_op jit(solution)/shard_map/all_to_all | solution.py:274
  185.0 0.7 second_own.1.refs_0_
  185.7 102.8 %all-to-all-done.recv = bf16[128,30,8,128]{3,2,1,0:T(8,128)(2,1)} async-done(((bf16[128,30,8,128]{3,2,1,0:T(8,128)(2,1)}), bf16[128,30,8,128]{3,2,1,0:T(8,128)(2,1)}, u32[]{:S(2)}, u32[]{:S(2)}) %all-to-all-start) | async-done | bytes 7864352 | tf_op jit(solution)/shard_map/all_to_all | solution.py:274
  288.5 81.3 %second_forward.1 = bf16[128,20,8,128]{3,2,1,0:T(8,128)(2,1)} custom-call(s32[1]{0:T(128)} %bitcast.me, s32[128]{0:T(128)} %partner.13, bf16[128,30,8,128]{3,2,1,0:T(8,128)(2,1)} %all-to-all-done.recv, bf16[128,20,8,128]{3,2,1,0:T(8,128)(2,1)} %second_own.1.refs_0_), custom_call_target="tpu_custom_call", output_to_operand_aliasing={{}: (3, {})} | custom-call | tf_op jit(solution)/shard_map/second_forward/pallas_call | solution.py:309
  369.8 7.0 all-to-all-start.1
  376.8 1.2 slice.20
  378.1 0.6 copy.29
  378.7 1.2 reshape.74
  379.9 2.7 slice_bitcast_fusion.1
  382.6 19.7 %fusion.4 = bf16[1536,768]{1,0:T(8,128)(2,1)S(1)} fusion(bf16[1,3072,768]{2,1,0:T(8,128)(2,1)} %param.19, bf16[1,768,3072]{2,1,0:T(8,128)(2,1)} %param.18, bf16[512,768]{1,0:T(8,128)(2,1)} %reshape.74, bf16[1024,768]{1,0:T(8,128)(2,1)} %slice_bitcast_fusion.1), kind=kOutput, calls=%fused_computation.4 | convolution fusion | flops 14510850048 | bytes 14155776 | tf_op jit(solution)/shard_map/dot_general | solution.py:328
  402.3 1.4 copy-done
  404.3 5.9 third_held.1.refs_1_
  410.4 1.6 pad_maximum_fusion.refs_0_
  412.0 27.9 %all-to-all-done.1.recv.recv2 = bf16[128,20,8,128]{3,2,1,0:T(8,128)(2,1)} async-done(((bf16[128,20,8,128]{3,2,1,0:T(8,128)(2,1)}), bf16[128,20,8,128]{3,2,1,0:T(8,128)(2,1)}, u32[]{:S(2)}, u32[]{:S(2)}) %all-to-all-start.1) | async-done | bytes 5242912 | tf_op jit(solution)/shard_map/all_to_all | solution.py:274
  439.9 152.7 %third_forward.1 = bf16[128,30,8,128]{3,2,1,0:T(8,128)(2,1)} custom-call(s32[1]{0:T(128)} %bitcast.me, s32[128]{0:T(128)} %partner.13, bf16[128,20,8,128]{3,2,1,0:T(8,128)(2,1)} %all-to-all-done.1.recv.recv2, bf16[128,9,8,128]{3,2,1,0:T(8,128)(2,1)} %pad_maximum_fusion.refs_0_, ...), custom_call_target="tpu_custom_call", output_to_operand_aliasing={{}: (4, {})} | custom-call | tf_op jit(solution)/shard_map/third_forward/pallas_call | solution.py:343
  592.6 8.5 all-to-all-start.2
  601.1 0.8 copy.26.gate_one
  601.9 0.8 copy.27.gate_two
  602.6 287.7 %settle.1 = (bf16[2304,8,128]{2,1,0:T(8,128)(2,1)}, bf16[2304,8,128]{2,1,0:T(8,128)(2,1)}) custom-call(s32[1]{0:T(128)} %bitcast.me, s32[128]{0:T(128)} %partner.13, bf16[2304,8,128]{2,1,0:T(8,128)(2,1)} %bitcast.52, bf16[2304,8,128]{2,1,0:T(8,128)(2,1)} %bitcast.55, bf16[128,20,8,128]{3,2,1,0:T(8,128)(2,1)} %all-to-all-done.1.recv.recv2), custom_call_target="tpu_custom_call" | custom-call | tf_op jit(solution)/shard_map/settle/pallas_call | solution.py:355
  890.3 5.4 last.1
  (12 shorter events, 0.8 us)
Async XLA Ops:
  10.4 278.1 %all-to-all-start = ((bf16[128,30,8,128]{3,2,1,0:T(8,128)(2,1)}), bf16[128,30,8,128]{3,2,1,0:T(8,128)(2,1)}, u32[]{:S(2)}, u32[]{:S(2)}) async-start(bf16[128,30,8,128]{3,2,1,0:T(8,128)(2,1)} %get-tuple-element.12), calls=%async_computation | async-start | bytes 15728640 | tf_op jit(solution)/shard_map/all_to_all | solution.py:274
  369.8 70.2 %all-to-all-start.1 = ((bf16[128,20,8,128]{3,2,1,0:T(8,128)(2,1)}), bf16[128,20,8,128]{3,2,1,0:T(8,128)(2,1)}, u32[]{:S(2)}, u32[]{:S(2)}) async-start(bf16[128,20,8,128]{3,2,1,0:T(8,128)(2,1)} %second_forward.1), calls=%async_computation.1 | async-start | bytes 10485760 | tf_op jit(solution)/shard_map/all_to_all | solution.py:274
  402.3 1.4 copy-start
  404.3 6.0 copy-start.1
  592.6 8.5 copy-start.2
  592.6 9.2 %copy-start.3 = (f32[192]{0:T(256)S(1)}, f32[192]{0:T(256)}, u32[]{:S(2)}) copy-start(f32[192]{0:T(256)} %param.16) | copy-start | bytes 2308
  592.6 297.7 %all-to-all-start.2 = ((bf16[128,30,8,128]{3,2,1,0:T(8,128)(2,1)}), bf16[128,30,8,128]{3,2,1,0:T(8,128)(2,1)}, u32[]{:S(2)}, u32[]{:S(2)}) async-start(bf16[128,30,8,128]{3,2,1,0:T(8,128)(2,1)} %third_forward.1), calls=%async_computation.2 | async-start | bytes 15728640 | tf_op jit(solution)/shard_map/all_to_all | solution.py:274

commit v2 on v1

v2 whole, which is shorter than its diff:
```python
import functools

import jax
import jax.numpy as jnp
from jax import lax
from jax.experimental import pallas as pl
from jax.experimental.pallas import tpu as pltpu
from jax.sharding import PartitionSpec as P

AXES = ("gx", "gy")
EPS = 1e-06
CAP = 6
N = 128
HALF = 2304
CHUNK = 72
TOK = 9
C1, C2, C3 = 21, 20, 21
NPART = 41
MA2 = 10
MB2 = C2 - MA2
GROUPS = 8
SIZE = N // GROUPS

HBM = pl.BlockSpec(memory_space=pltpu.MemorySpace.HBM)
SMEM = pl.BlockSpec(memory_space=pltpu.SMEM)
VMEM = pl.BlockSpec(memory_space=pltpu.VMEM)
BF = jnp.bfloat16


def tiles_of(w, rows, cols):
    return w.reshape(rows // 8, 8, cols // 128, 128).transpose(0, 2, 1, 3).reshape(HALF, 8, 128)


def array_of(t, rows, cols):
    return t.reshape(rows // 8, cols // 128, 8, 128).transpose(0, 2, 1, 3).reshape(1, rows, cols)


def copies(partner, visit, after=None):
    def step(j, counts):
        movers, stayers = counts
        p = partner[j]
        moving = p != j
        visit(j, moving, jnp.where(moving, movers, stayers), p)
        one = moving.astype(jnp.int32)
        return (movers + one, stayers + 1 - one)

    def group(g, counts):
        counts = lax.fori_loop(g * SIZE, (g + 1) * SIZE, step, counts)
        if after is not None:
            after(g)
        return counts

    lax.fori_loop(0, GROUPS, group, (jnp.int32(0), jnp.int32(0)))


def own_piece(w_in, w_out, rank, offset, size, act):
    @pl.when(rank < 32)
    def _():
        act(w_in.at[pl.ds(rank * CHUNK + offset, size)])

    @pl.when(rank >= 32)
    def _():
        act(w_out.at[pl.ds((rank - 32) * CHUNK + offset, size)])


def go(src, dst, sem, wait):
    copy = pltpu.make_async_copy(src, dst, sem)
    if wait:
        copy.wait()
    else:
        copy.start()


def nothing(j, moving, rank, p):
    pass


def column(row):
    n = row.shape[1]
    eye = lax.broadcasted_iota(jnp.int32, (n, n), 0) == lax.broadcasted_iota(jnp.int32, (n, n), 1)
    return jnp.sum(jnp.where(eye, row, 0), axis=1, keepdims=True)


def first_kernel(
    me, partner, w_in, w_out, one, two, routes_one, routes_two, gain, place,
    buf1, pos, stage, sem, osem,
):
    my = me[0]
    i_move = partner[my] != my

    def visit(wait, j, moving, rank, p):
        offset = jnp.where(moving, NPART, 0)
        own_piece(
            w_in, w_out, rank, offset, C1,
            lambda src: go(src, stage.at[j, pl.ds(0, C1)], sem.at[j // SIZE], wait),
        )

    @pl.when(i_move)
    def _():
        copies(partner, functools.partial(visit, False))

    rows = one.shape[0]
    width = one.shape[1]
    cols = width // 128
    total = 2 * rows
    slots = place[...]
    lower = (
        lax.broadcasted_iota(jnp.int32, (rows, rows), 1)
        < lax.broadcasted_iota(jnp.int32, (rows, rows), 0)
    ).astype(jnp.float32).astype(BF)
    lane = lax.broadcasted_iota(jnp.int32, (rows, N), 1)
    normed, target, place_in = [], [], []
    for b, (group, routes) in enumerate(((one, routes_one), (two, routes_two))):
        values = group[...].astype(jnp.float32)
        scaling = lax.rsqrt(jnp.mean(values * values, axis=1, keepdims=True) + EPS)
        normed.append((values * scaling * gain[...]).astype(BF))
        member = column(routes[...]) == slots
        flag = member.astype(jnp.float32)
        before = jnp.dot(lower, flag.astype(BF), preferred_element_type=jnp.float32)
        target.append(jnp.sum(jnp.where(member, lane, 0), axis=1, keepdims=True))
        place_in.append(
            jnp.sum(flag * before, axis=1, keepdims=True).astype(jnp.int32) + b * CAP
        )
    normed = jnp.concatenate(normed, axis=0)
    target = jnp.concatenate(target, axis=0)
    place_in = jnp.concatenate(place_in, axis=0)
    early = jnp.where(place_in < 8, target * 8 + place_in, -1)
    late = jnp.where(place_in < 8, -1, target * 8 + place_in - 8)
    pos[:, 0:1] = early
    pos[:, 1:2] = late

    def out(wait, lo, size, g):
        part = pl.ds(g * SIZE, SIZE)
        go(stage.at[part, pl.ds(lo, size)], buf1.at[part, pl.ds(lo, size)], osem, wait)

    @pl.when(i_move)
    def _():
        copies(partner, functools.partial(visit, True), functools.partial(out, False, 0, C1))

    eye = lax.broadcasted_iota(jnp.int32, (total, total), 0) == lax.broadcasted_iota(
        jnp.int32, (total, total), 1
    )
    early_row = jnp.sum(jnp.where(eye, early, 0), axis=0, keepdims=True)
    late_row = jnp.sum(jnp.where(eye, late, 0), axis=0, keepdims=True)
    row = lax.broadcasted_iota(jnp.int32, (N * 8, total), 0)
    pick = (row == early_row).astype(jnp.float32).astype(BF)
    top = jnp.dot(pick, normed, preferred_element_type=jnp.float32)
    fours = row - (row & 4)
    pick = (fours == late_row).astype(jnp.float32).astype(BF)
    rest = jnp.dot(pick, normed, preferred_element_type=jnp.float32)
    upper = lax.broadcasted_iota(jnp.int32, (N, 8, 128), 1) < 4
    cut = lambda x, c: x[:, c * 128 : (c + 1) * 128].reshape(N, 8, 128)
    for c in range(cols):
        stage[:, C1 + c] = cut(top, c).astype(BF)
    for c in range(cols // 2):
        stage[:, C1 + cols + c] = jnp.where(upper, cut(rest, 2 * c), cut(rest, 2 * c + 1)).astype(BF)
    for g in range(GROUPS):
        out(False, C1, TOK, g)
    for g in range(GROUPS):
        out(True, C1, TOK, g)

    @pl.when(i_move)
    def _():
        copies(partner, nothing, functools.partial(out, True, 0, C1))


def second_kernel(me, partner, w_in, w_out, recv1, buf2, stage, sem, osem):
    my = me[0]
    i_move = partner[my] != my

    def from_mover(wait, j, moving, rank, p):
        at = sem.at[j // SIZE]

        @pl.when(moving)
        def _():
            own_piece(
                w_in, w_out, rank, NPART + C1, MA2,
                lambda src: go(src, stage.at[j, pl.ds(0, MA2)], at, wait),
            )
            go(recv1.at[p, pl.ds(0, MB2)], stage.at[j, pl.ds(MA2, MB2)], at, wait)

        @pl.when(jnp.logical_not(moving))
        def _():
            own_piece(
                w_in, w_out, rank, C1, C2,
                lambda src: go(src, stage.at[j, pl.ds(0, C2)], at, wait),
            )

    def from_stayer(wait, j, moving, rank, p):
        @pl.when(moving)
        def _():
            go(recv1.at[p, pl.ds(0, C2)], stage.at[j, pl.ds(0, C2)], sem.at[j // SIZE], wait)

    def out(wait, g):
        part = pl.ds(g * SIZE, SIZE)
        go(stage.at[part], buf2.at[part], osem, wait)

    for mine, visit in ((True, from_mover), (False, from_stayer)):
        @pl.when(i_move == mine)
        def _():
            copies(partner, functools.partial(visit, False))
            copies(partner, functools.partial(visit, True), functools.partial(out, False))
            copies(partner, nothing, functools.partial(out, True))


def third_kernel(me, partner, recv1, recv2, answers, buf3, stage, sem, osem):
    my = me[0]
    i_move = partner[my] != my

    def visit(early, late, wait, j, moving, rank, p):
        at = sem.at[j // SIZE]

        @pl.when(moving)
        def _():
            go(recv1.at[p, pl.ds(early, C1 - late)], stage.at[j, pl.ds(0, C1 - late)], at, wait)
            go(recv2.at[p, pl.ds(0, late)], stage.at[j, pl.ds(C1 - late, late)], at, wait)

    def token(wait, g):
        part = pl.ds(g * SIZE, SIZE)
        go(answers.at[part], stage.at[part, pl.ds(C3, TOK)], sem.at[g], wait)

    def out(wait, g):
        part = pl.ds(g * SIZE, SIZE)
        if not wait:
            token(True, g)
        go(stage.at[part], buf3.at[part], osem, wait)

    for mine, early, late in ((True, MB2, MA2), (False, C2, C2)):
        step = functools.partial(visit, early, late)

        @pl.when(i_move == mine)
        def _():
            copies(partner, functools.partial(step, False), functools.partial(token, False))
            copies(partner, functools.partial(step, True), functools.partial(out, False))
            copies(partner, nothing, functools.partial(out, True))


def settle_kernel(me, partner, w_in, w_out, recv2, new_in, new_out, stage, sem, osem):
    my = me[0]
    i_move = partner[my] != my

    def load(wait, g):
        part = pl.ds(g * SIZE * C2, SIZE * C2)
        go(recv2.at[part], stage.at[part], sem.at[g], wait)

    def visit(wait, j, moving, rank, p):
        if not wait:
            @pl.when(j % SIZE == 0)
            def _():
                load(True, j // SIZE)

        @pl.when(moving)
        def _():
            own_piece(
                new_in, new_out, rank, NPART, MB2,
                lambda dst: go(stage.at[pl.ds(j * C2 + MA2, MB2)], dst, osem, wait),
            )

        @pl.when(jnp.logical_not(moving))
        def _():
            own_piece(
                new_in, new_out, rank, 0, C2,
                lambda dst: go(stage.at[pl.ds(j * C2, C2)], dst, osem, wait),
            )

    @pl.when(i_move)
    def _():
        copies(partner, nothing, functools.partial(load, False))
        copies(partner, functools.partial(visit, False))
        copies(partner, functools.partial(visit, True))

    @pl.when(jnp.logical_not(i_move))
    def _():
        size = HALF // GROUPS
        pieces = [
            (src.at[pl.ds(g * size, size)], stage.at[pl.ds(h * HALF + g * size, size)],
             dst.at[pl.ds(g * size, size)], g)
            for h, (src, dst) in enumerate(((w_in, new_in), (w_out, new_out)))
            for g in range(GROUPS)
        ]
        for h in range(2):
            half = pieces[h * GROUPS : (h + 1) * GROUPS]
            for src, mid, dst, g in half:
                go(src, mid, sem.at[g], False)
            for src, mid, dst, g in half:
                go(src, mid, sem.at[g], True)
                go(mid, dst, osem, False)
        for src, mid, dst, g in pieces:
            go(mid, dst, osem, True)


def last_kernel(
    me, partner, recv3, pos, one, two, gate_one, gate_two, in_, out_,
    res_one, res_two, new_in, new_out, stage, sem, osem,
):
    my = me[0]
    i_move = partner[my] != my

    def load(wait, g):
        part = pl.ds(g * SIZE, SIZE)
        go(recv3.at[part], stage.at[part], sem.at[g], wait)

    def visit(wait, j, moving, rank, p):
        offset = jnp.where(moving, NPART + MB2, C2)
        own_piece(
            new_in, new_out, rank, offset, C3,
            lambda dst: go(stage.at[j, pl.ds(0, C3)], dst, osem, wait),
        )

    for g in range(GROUPS):
        load(False, g)
    for g in range(GROUPS):
        load(True, g)

    @pl.when(i_move)
    def _():
        copies(partner, functools.partial(visit, False))

    rows = one.shape[0]
    width = one.shape[1]
    cols = width // 128
    total = 2 * rows
    early = pos[:, 0:1]
    late = pos[:, 1:2]
    lane = lax.broadcasted_iota(jnp.int32, (total, N * 8), 1)
    hot = lambda where: (lane == where).astype(jnp.float32).astype(BF)
    flat = lambda c: stage[:, C3 + c].astype(jnp.float32).reshape(N * 8, 128).astype(BF)
    full = jnp.concatenate([flat(c) for c in range(cols)], axis=1)
    tail = jnp.concatenate([flat(cols + c) for c in range(cols // 2)], axis=1)
    top = jnp.dot(hot(early), full, preferred_element_type=jnp.float32)
    even = jnp.dot(hot(late), tail, preferred_element_type=jnp.float32)
    odd = jnp.dot(
        hot(jnp.where(late < 0, -1, late + 4)), tail, preferred_element_type=jnp.float32
    )
    for b, (group, gate, res) in enumerate(
        ((one, gate_one, res_one), (two, gate_two, res_two))
    ):
        r = slice(b * rows, (b + 1) * rows)
        for c in range(cols):
            s = slice(c * 128, (c + 1) * 128)
            h = slice(c // 2 * 128, (c // 2 + 1) * 128)
            answer = top[r, s] + (odd if c % 2 else even)[r, h]
            res[:, s] = (group[:, s].astype(jnp.float32) + gate[...] * answer).astype(BF)

    @pl.when(i_move)
    def _():
        copies(partner, functools.partial(visit, True))


def shape(*dims, dtype=BF):
    return jax.ShapeDtypeStruct(dims, dtype)


def exchange(x):
    return lax.all_to_all(x, AXES, split_axis=0, concat_axis=0, tiled=True)


DMA = pltpu.SemaphoreType.DMA(())
SEMS = pltpu.SemaphoreType.DMA((GROUPS,))


def local(
    group_one, routes_one, gates_one, group_two, routes_two, gates_two,
    norm_gain, weight_in, weight_out, old_place, partner,
):
    rows, width = group_one.shape
    ff = weight_in.shape[2]
    me = lax.axis_index(AXES).astype(jnp.int32).reshape(1)
    w_in = tiles_of(weight_in, width, ff)
    w_out = tiles_of(weight_out, ff, width)
    buf1, pos = pl.pallas_call(
        first_kernel,
        out_shape=(shape(N, C1 + TOK, 8, 128), shape(2 * rows, 2, dtype=jnp.int32)),
        in_specs=[SMEM, SMEM, HBM, HBM] + [VMEM] * 6,
        out_specs=(HBM, VMEM),
        scratch_shapes=[pltpu.VMEM((N, C1 + TOK, 8, 128), BF), SEMS, DMA],
        name="first",
    )(
        me, partner, w_in, w_out, group_one, group_two,
        routes_one.reshape(1, rows), routes_two.reshape(1, rows),
        norm_gain.reshape(1, width), old_place.reshape(1, N),
    )
    recv1 = exchange(buf1)
    buf2 = pl.pallas_call(
        second_kernel,
        out_shape=shape(N, C2, 8, 128),
        in_specs=[SMEM, SMEM, HBM, HBM, HBM],
        out_specs=HBM,
        scratch_shapes=[pltpu.VMEM((N, C2, 8, 128), BF), SEMS, DMA],
        name="second",
    )(me, partner, w_in, w_out, recv1)
    recv2 = exchange(buf2)
    arrived = recv1[:, C1:]
    cols = width // 128
    top = arrived[:, :cols].transpose(0, 2, 1, 3).reshape(N * 8, width)
    rest = arrived[:, cols:].reshape(N, cols // 2, 2, 4, 128)
    rest = rest.transpose(0, 3, 1, 2, 4).reshape(N * 4, width)
    inputs = jnp.concatenate([top, rest], axis=0)
    hidden = jnp.maximum(
        jnp.dot(inputs, weight_in[0], preferred_element_type=jnp.float32), 0.0
    ).astype(BF)
    result = jnp.dot(hidden, weight_out[0], preferred_element_type=jnp.float32).astype(BF)
    top = result[: N * 8].reshape(N, 8, cols, 128).transpose(0, 2, 1, 3)
    rest = result[N * 8 :].reshape(N, 4, cols // 2, 2, 128)
    rest = rest.transpose(0, 2, 3, 1, 4).reshape(N, cols // 2, 8, 128)
    answers = jnp.concatenate([top, rest], axis=1)
    buf3 = pl.pallas_call(
        third_kernel,
        out_shape=shape(N, C3 + TOK, 8, 128),
        in_specs=[SMEM, SMEM, HBM, HBM, pl.BlockSpec(memory_space=pl.ANY)],
        out_specs=HBM,
        scratch_shapes=[pltpu.VMEM((N, C3 + TOK, 8, 128), BF), SEMS, DMA],
        name="third",
    )(me, partner, recv1, recv2, answers)
    recv3 = exchange(buf3)
    new_in, new_out = pl.pallas_call(
        settle_kernel,
        out_shape=(shape(HALF, 8, 128), shape(HALF, 8, 128)),
        in_specs=[SMEM, SMEM, HBM, HBM, HBM],
        out_specs=(HBM, HBM),
        scratch_shapes=[pltpu.VMEM((2 * HALF, 8, 128), BF), SEMS, DMA],
        name="settle",
    )(me, partner, w_in, w_out, recv2.reshape(N * C2, 8, 128))
    res_one, res_two, new_in, new_out = pl.pallas_call(
        last_kernel,
        out_shape=(
            shape(rows, width), shape(rows, width), shape(HALF, 8, 128), shape(HALF, 8, 128),
        ),
        in_specs=[SMEM, SMEM, HBM] + [VMEM] * 5 + [HBM, HBM],
        out_specs=(VMEM, VMEM, HBM, HBM),
        scratch_shapes=[pltpu.VMEM((N, C3 + TOK, 8, 128), BF), SEMS, DMA],
        input_output_aliases={8: 2, 9: 3},
        name="last",
    )(
        me, partner, recv3, pos, group_one, group_two,
        gates_one.reshape(rows, 1), gates_two.reshape(rows, 1), new_in, new_out,
    )
    return (res_one, res_two, array_of(new_in, width, ff), array_of(new_out, ff, width))


def solution(mesh):
    split = P(AXES, None)
    flat = P(AXES)
    deep = P(AXES, None, None)
    return jax.shard_map(
        local,
        mesh=mesh,
        in_specs=(split, split, flat, split, split, flat, P(), deep, deep, P(), P()),
        out_specs=(split, split, deep, deep),
        check_vma=False,
    )
```

time: 898 us -> 323 us (0.36)
  Pallas kernels: 539 us -> 39.4 us
  starting transfers between devices: 190 us -> 15.7 us
  blocking collectives: 0 us -> 106 us
    pallas_call x5 -> x3, Pallas kernels: 528 us -> 19.2 us  [the longest x1 6.77 us: local(): pl.pallas_call(second_kernel, out_shape=shape(N, C2, 8, 128), in_specs=[S...]
    all_to_all x3 -> x2, starting transfers between devices: 190 us -> 15.7 us  [exchange(): return lax.all_to_all(x, AXES, split_axis=0, concat_axis=0, tiled=True)]
    all_to_all x0 -> x1, blocking collectives: none -> 106 us  [exchange(): return lax.all_to_all(x, AXES, split_axis=0, concat_axis=0, tiled=True)]
    all_to_all x3 -> x2, waiting for transfers between devices: 131 us -> 131 us  [exchange(): return lax.all_to_all(x, AXES, split_axis=0, concat_axis=0, tiled=True)]
  transfers between devices with their start and end apart: 3 -> 2, of which waited for: 2 -> 2; matrix products, arithmetic and copies ran while one was open for 3% -> 9% of each run, Pallas kernels for 33% -> 2%
where the time goes in v2:
time: 323 us
  waiting for transfers between devices  131 us (41%)
  blocking collectives  106 us (33%)
  Pallas kernels  39.4 us (12%)
  matrix products  20.5 us (6%)
  starting transfers between devices  15.7 us (5%)
  local copies, waits for them, and re-layouts  8.63 us (3%)
    all_to_all x2, waiting for transfers between devices, exchange(): return lax.all_to_all(x, AXES, split_axis=0, concat_axis=0, tiled=True)  131 us
    all_to_all x1, blocking collectives, exchange(): return lax.all_to_all(x, AXES, split_axis=0, concat_axis=0, tiled=True)  106 us
    dot_general x1, matrix products, local(): jnp.dot(hidden, weight_out[0], preferred_element_type=jnp.float32)  20.5 us
    all_to_all x2, starting transfers between devices, exchange(): return lax.all_to_all(x, AXES, split_axis=0, concat_axis=0, tiled=True)  15.7 us
    pallas_call x1, Pallas kernels, local(): pl.pallas_call(last_kernel, out_shape=(shape(rows, width), shape(rows, wi...  10.3 us
    pallas_call x1, Pallas kernels, local(): pl.pallas_call(first_kernel, out_shape=(shape(N, C1 + TOK, 8, 128), shape...  9.98 us
    pallas_call x1, Pallas kernels, local(): pl.pallas_call(second_kernel, out_shape=shape(N, C2, 8, 128), in_specs=[S...  6.77 us
    pallas_call x1, Pallas kernels, local(): pl.pallas_call(settle_kernel, out_shape=(shape(HALF, 8, 128), shape(HALF,...  6.47 us
  transfers between devices with their start and end apart: 2, of which 2 were waited for; matrix products, arithmetic and copies ran while one was open for 9% of the time, Pallas kernels for 2%

profile of v2, /device:TPU:37, one launch (start us, length us, event | category | flops | bytes accessed | tf_op | source)
XLA Modules:
  0.0 323.2 jit_solution(12763660702187457552)
XLA Ops:
  0.6 1.3 reshape.81.gain
  1.9 10.0 %first.1 = (bf16[128,30,8,128]{3,2,1,0:T(8,128)(2,1)}, s32[384,2]{1,0:T(8,128)}) custom-call(s32[1]{0:T(128)} %bitcast.me, s32[128]{0:T(128)} %partner.9, bf16[2304,8,128]{2,1,0:T(8,128)(2,1)} %bitcast.54, bf16[2304,8,128]{2,1,0:T(8,128)(2,1)} %bitcast.57, bf16[192,768]{1,0:T(8,128)(2,1)} %one.3, bf16[192,768]{1,0:T(8,128)(2,1)} %two.3, s32[1,192]{1,0:T(1,128)} %bitcast.66, ...), custom_call_target="tpu_custom_call" | custom-call | tf_op jit(solution)/shard_map/first/pallas_call | solution.py:371
  11.9 105.6 %all_to_all.15.recv1 = bf16[128,30,8,128]{3,2,1,0:T(8,128)(2,1)} all-to-all(bf16[128,30,8,128]{3,2,1,0:T(8,128)(2,1)} %get-tuple-element.12), channel_id=1, replica_groups=mesh['gx'=8,'gy'=16] {'gx','gy'}, dimensions={0} | all-to-all | bytes 15728640 | tf_op jit(solution)/shard_map/all_to_all | solution.py:355
  117.5 6.8 %second.1 = bf16[128,20,8,128]{3,2,1,0:T(8,128)(2,1)} custom-call(s32[1]{0:T(128)} %bitcast.me, s32[128]{0:T(128)} %partner.9, bf16[2304,8,128]{2,1,0:T(8,128)(2,1)} %bitcast.55, bf16[2304,8,128]{2,1,0:T(8,128)(2,1)} %bitcast.58, bf16[128,30,8,128]{3,2,1,0:T(8,128)(2,1)} %all_to_all.15.recv1), custom_call_target="tpu_custom_call" | custom-call | tf_op jit(solution)/shard_map/second/pallas_call | solution.py:384
  124.3 7.4 %all-to-all-start.1 = ((bf16[128,20,8,128]{3,2,1,0:T(8,128)(2,1)}), bf16[128,20,8,128]{3,2,1,0:T(8,128)(2,1)}, u32[]{:S(2)}, u32[]{:S(2)}) async-start(bf16[128,20,8,128]{3,2,1,0:T(8,128)(2,1)} %second.1), calls=%async_computation.1 | async-start | bytes 10485760 | tf_op jit(solution)/shard_map/all_to_all | solution.py:355
  131.7 0.6 copy.23
  132.3 0.4 reshape.85
  132.7 1.5 slice_bitcast_fusion.1
  134.2 20.5 %fusion.4 = bf16[1536,768]{1,0:T(8,128)(2,1)} fusion(bf16[1,3072,768]{2,1,0:T(8,128)(2,1)} %param.19, bf16[1,768,3072]{2,1,0:T(8,128)(2,1)} %param.18, bf16[512,768]{1,0:T(8,128)(2,1)S(1)} %reshape.85, bf16[1024,768]{1,0:T(8,128)(2,1)S(1)} %slice_bitcast_fusion.1), kind=kOutput, calls=%fused_computation.4 | convolution fusion | flops 14510850048 | bytes 14155776 | tf_op jit(solution)/shard_map/dot_general | solution.py:402
  154.7 1.2 slice.22
  155.8 0.2 reshape.87
  156.0 0.4 copy.19
  156.4 1.5 slice_bitcast_fusion
  158.0 1.6 pad_maximum_fusion.answers
  159.6 35.3 %all-to-all-done.1.recv2 = bf16[128,20,8,128]{3,2,1,0:T(8,128)(2,1)} async-done(((bf16[128,20,8,128]{3,2,1,0:T(8,128)(2,1)}), bf16[128,20,8,128]{3,2,1,0:T(8,128)(2,1)}, u32[]{:S(2)}, u32[]{:S(2)}) %all-to-all-start.1) | async-done | bytes 5242912 | tf_op jit(solution)/shard_map/all_to_all | solution.py:355
  194.8 5.9 %third.1 = bf16[128,30,8,128]{3,2,1,0:T(8,128)(2,1)} custom-call(s32[1]{0:T(128)} %bitcast.me, s32[128]{0:T(128)} %partner.9, bf16[128,30,8,128]{3,2,1,0:T(8,128)(2,1)} %all_to_all.15.recv1, bf16[128,20,8,128]{3,2,1,0:T(8,128)(2,1)} %all-to-all-done.1.recv2, bf16[128,9,8,128]{3,2,1,0:T(8,128)(2,1)} %pad_maximum_fusion.answers), custom_call_target="tpu_custom_call" | custom-call | tf_op jit(solution)/shard_map/third/pallas_call | solution.py:407
  200.8 0.0 copy-start
  200.8 0.0 copy-start.1
  200.8 8.4 %all-to-all-start.2 = ((bf16[128,30,8,128]{3,2,1,0:T(8,128)(2,1)}), bf16[128,30,8,128]{3,2,1,0:T(8,128)(2,1)}, u32[]{:S(2)}, u32[]{:S(2)}) async-start(bf16[128,30,8,128]{3,2,1,0:T(8,128)(2,1)} %third.1), calls=%async_computation.2 | async-start | bytes 15728640 | tf_op jit(solution)/shard_map/all_to_all | solution.py:355
  209.2 0.8 copy.20.gate_one
  210.0 0.8 copy.21.gate_two
  210.8 6.5 %settle.1 = (bf16[2304,8,128]{2,1,0:T(8,128)(2,1)}, bf16[2304,8,128]{2,1,0:T(8,128)(2,1)}) custom-call(s32[1]{0:T(128)} %bitcast.me, s32[128]{0:T(128)} %partner.9, bf16[2304,8,128]{2,1,0:T(8,128)(2,1)} %bitcast.56, bf16[2304,8,128]{2,1,0:T(8,128)(2,1)} %bitcast.59, bf16[2560,8,128]{2,1,0:T(8,128)(2,1)} %bitcast.26.recv2), custom_call_target="tpu_custom_call" | custom-call | tf_op jit(solution)/shard_map/settle/pallas_call | solution.py:416
  217.2 95.5 %all-to-all-done.2.recv3 = bf16[128,30,8,128]{3,2,1,0:T(8,128)(2,1)} async-done(((bf16[128,30,8,128]{3,2,1,0:T(8,128)(2,1)}), bf16[128,30,8,128]{3,2,1,0:T(8,128)(2,1)}, u32[]{:S(2)}, u32[]{:S(2)}) %all-to-all-start.2) | async-done | bytes 7864352 | tf_op jit(solution)/shard_map/all_to_all | solution.py:355
  312.7 10.3 %last.1 = (bf16[192,768]{1,0:T(8,128)(2,1)}, bf16[192,768]{1,0:T(8,128)(2,1)}, bf16[2304,8,128]{2,1,0:T(8,128)(2,1)}, bf16[2304,8,128]{2,1,0:T(8,128)(2,1)}) custom-call(s32[1]{0:T(128)} %bitcast.me, s32[128]{0:T(128)} %partner.9, bf16[128,30,8,128]{3,2,1,0:T(8,128)(2,1)} %all-to-all-done.2.recv3, ...), custom_call_target="tpu_custom_call", output_to_operand_aliasing={{2}: (8, {}), {3}: (9, {})} | custom-call | tf_op jit(solution)/shard_map/last/pallas_call | solution.py:424
  (4 shorter events, 0.0 us)
Async XLA Ops:
  124.3 7.4 %slice-start = ((bf16[128,30,8,128]{3,2,1,0:T(8,128)(2,1)}), bf16[128,3,8,128]{3,2,1,0:T(8,128)(2,1)S(1)}, s32[]{:S(2)}) async-start(bf16[128,30,8,128]{3,2,1,0:T(8,128)(2,1)} %all_to_all.15.recv1), calls=%async_computation.3 | async-start | bytes 1572864 | tf_op jit(solution)/shard_map/slice | solution.py:396
  124.3 70.6 %all-to-all-start.1 = ((bf16[128,20,8,128]{3,2,1,0:T(8,128)(2,1)}), bf16[128,20,8,128]{3,2,1,0:T(8,128)(2,1)}, u32[]{:S(2)}, u32[]{:S(2)}) async-start(bf16[128,20,8,128]{3,2,1,0:T(8,128)(2,1)} %second.1), calls=%async_computation.1 | async-start | bytes 10485760 | tf_op jit(solution)/shard_map/all_to_all | solution.py:355
  200.8 8.4 %copy-start = (f32[192]{0:T(256)S(1)}, f32[192]{0:T(256)}, u32[]{:S(2)}) copy-start(f32[192]{0:T(256)} %param.13) | copy-start | bytes 2308
  200.8 9.2 %copy-start.1 = (f32[192]{0:T(256)S(1)}, f32[192]{0:T(256)}, u32[]{:S(2)}) copy-start(f32[192]{0:T(256)} %param.16) | copy-start | bytes 2308
  200.8 111.9 %all-to-all-start.2 = ((bf16[128,30,8,128]{3,2,1,0:T(8,128)(2,1)}), bf16[128,30,8,128]{3,2,1,0:T(8,128)(2,1)}, u32[]{:S(2)}, u32[]{:S(2)}) async-start(bf16[128,30,8,128]{3,2,1,0:T(8,128)(2,1)} %third.1), calls=%async_computation.2 | async-start | bytes 15728640 | tf_op jit(solution)/shard_map/all_to_all | solution.py:355

commit v3 on v2

--- a/solution.py
+++ b/solution.py
@@ -20,6 +20,7 @@
 MB2 = C2 - MA2
 GROUPS = 8
 SIZE = N // GROUPS
+UNROLL = 4
 
 HBM = pl.BlockSpec(memory_space=pltpu.MemorySpace.HBM)
 SMEM = pl.BlockSpec(memory_space=pltpu.SMEM)
@@ -81,23 +82,51 @@
     return jnp.sum(jnp.where(eye, row, 0), axis=1, keepdims=True)
 
 
+def both_halves(step, w_in, w_out):
+    half = N // 4
+    lax.fori_loop(0, half, lambda k, c: (step(k, w_in, k * CHUNK), c)[1], 0, unroll=UNROLL)
+    lax.fori_loop(
+        0, half, lambda k, c: (step(k + half, w_out, k * CHUNK), c)[1], 0, unroll=UNROLL
+    )
+
+
+def each_mover(step):
+    lax.fori_loop(0, N // 2, lambda k, c: (step(k), c)[1], 0, unroll=UNROLL)
+
+
+def settled(ref, sem):
+    pltpu.make_async_copy(ref, ref, sem).wait()
+
+
+def group_of(g):
+    return pl.ds(g * SIZE, SIZE)
+
+
 def first_kernel(
     me, partner, w_in, w_out, one, two, routes_one, routes_two, gain, place,
-    buf1, pos, stage, sem, osem,
+    buf1, pos, order, stage, sem, osem,
 ):
     my = me[0]
     i_move = partner[my] != my
 
-    def visit(wait, j, moving, rank, p):
-        offset = jnp.where(moving, NPART, 0)
-        own_piece(
-            w_in, w_out, rank, offset, C1,
-            lambda src: go(src, stage.at[j, pl.ds(0, C1)], sem.at[j // SIZE], wait),
-        )
-
-    @pl.when(i_move)
-    def _():
-        copies(partner, functools.partial(visit, False))
+    def sort(j, counts):
+        movers, stayers = counts
+        moving = partner[j] != j
+        order[jnp.where(moving, movers, stayers)] = j
+        one = moving.astype(jnp.int32)
+        return (movers + one, stayers + 1 - one)
+
+    lax.fori_loop(0, N, sort, (jnp.int32(0), jnp.int32(N // 2)), unroll=UNROLL)
+
+    @pl.when(i_move)
+    def _():
+        def step(k, w, tile):
+            m = order[k]
+            t = order[k + N // 2]
+            go(w.at[pl.ds(tile, C1)], stage.at[t, pl.ds(0, C1)], sem.at[t // SIZE], False)
+            go(w.at[pl.ds(tile + NPART, C1)], stage.at[m, pl.ds(0, C1)], sem.at[m // SIZE], False)
+
+        both_halves(step, w_in, w_out)
 
     rows = one.shape[0]
     width = one.shape[1]
@@ -109,11 +138,12 @@
         < lax.broadcasted_iota(jnp.int32, (rows, rows), 0)
     ).astype(jnp.float32).astype(BF)
     lane = lax.broadcasted_iota(jnp.int32, (rows, N), 1)
+    scale = jnp.concatenate([gain[c : c + 1, :] for c in range(cols)], axis=1)
     normed, target, place_in = [], [], []
     for b, (group, routes) in enumerate(((one, routes_one), (two, routes_two))):
         values = group[...].astype(jnp.float32)
         scaling = lax.rsqrt(jnp.mean(values * values, axis=1, keepdims=True) + EPS)
-        normed.append((values * scaling * gain[...]).astype(BF))
+        normed.append((values * scaling * scale).astype(BF))
         member = column(routes[...]) == slots
         flag = member.astype(jnp.float32)
         before = jnp.dot(lower, flag.astype(BF), preferred_element_type=jnp.float32)
@@ -129,13 +159,18 @@
     pos[:, 0:1] = early
     pos[:, 1:2] = late
 
-    def out(wait, lo, size, g):
-        part = pl.ds(g * SIZE, SIZE)
-        go(stage.at[part, pl.ds(lo, size)], buf1.at[part, pl.ds(lo, size)], osem, wait)
-
-    @pl.when(i_move)
-    def _():
-        copies(partner, functools.partial(visit, True), functools.partial(out, False, 0, C1))
+    def tiles(lo, size):
+        go(stage.at[:, pl.ds(lo, size)], buf1.at[:, pl.ds(lo, size)], osem, False)
+
+    def out(lo, size, g):
+        part = group_of(g)
+        go(stage.at[part, pl.ds(lo, size)], buf1.at[part, pl.ds(lo, size)], osem, False)
+
+    @pl.when(i_move)
+    def _():
+        for g in range(GROUPS):
+            settled(stage.at[group_of(g), pl.ds(0, C1)], sem.at[g])
+            out(0, C1, g)
 
     eye = lax.broadcasted_iota(jnp.int32, (total, total), 0) == lax.broadcasted_iota(
         jnp.int32, (total, total), 1
@@ -143,96 +178,98 @@
     early_row = jnp.sum(jnp.where(eye, early, 0), axis=0, keepdims=True)
     late_row = jnp.sum(jnp.where(eye, late, 0), axis=0, keepdims=True)
     row = lax.broadcasted_iota(jnp.int32, (N * 8, total), 0)
+    fours = row - (row & 4)
+    upper = lax.broadcasted_iota(jnp.int32, (N, 8, 128), 1) < 4
+    cut = lambda x, c: x[:, c * 128 : (c + 1) * 128].reshape(N, 8, 128)
+    pick = (fours == late_row).astype(jnp.float32).astype(BF)
+    rest = jnp.dot(pick, normed, preferred_element_type=jnp.float32)
+    for c in range(cols // 2):
+        stage[:, C1 + cols + c] = jnp.where(upper, cut(rest, 2 * c), cut(rest, 2 * c + 1)).astype(BF)
+    tiles(C1 + cols, cols // 2)
     pick = (row == early_row).astype(jnp.float32).astype(BF)
     top = jnp.dot(pick, normed, preferred_element_type=jnp.float32)
-    fours = row - (row & 4)
-    pick = (fours == late_row).astype(jnp.float32).astype(BF)
-    rest = jnp.dot(pick, normed, preferred_element_type=jnp.float32)
-    upper = lax.broadcasted_iota(jnp.int32, (N, 8, 128), 1) < 4
-    cut = lambda x, c: x[:, c * 128 : (c + 1) * 128].reshape(N, 8, 128)
     for c in range(cols):
         stage[:, C1 + c] = cut(top, c).astype(BF)
-    for c in range(cols // 2):
-        stage[:, C1 + cols + c] = jnp.where(upper, cut(rest, 2 * c), cut(rest, 2 * c + 1)).astype(BF)
-    for g in range(GROUPS):
-        out(False, C1, TOK, g)
-    for g in range(GROUPS):
-        out(True, C1, TOK, g)
-
-    @pl.when(i_move)
-    def _():
-        copies(partner, nothing, functools.partial(out, True, 0, C1))
-
-
-def second_kernel(me, partner, w_in, w_out, recv1, buf2, stage, sem, osem):
+    tiles(C1, cols)
+    settled(stage.at[:, pl.ds(C1, TOK)], osem)
+
+    @pl.when(i_move)
+    def _():
+        settled(stage.at[:, pl.ds(0, C1)], osem)
+
+
+def second_kernel(me, partner, order, w_in, w_out, recv1, buf2, stage, sem, osem):
     my = me[0]
     i_move = partner[my] != my
 
-    def from_mover(wait, j, moving, rank, p):
-        at = sem.at[j // SIZE]
-
-        @pl.when(moving)
-        def _():
-            own_piece(
-                w_in, w_out, rank, NPART + C1, MA2,
-                lambda src: go(src, stage.at[j, pl.ds(0, MA2)], at, wait),
-            )
-            go(recv1.at[p, pl.ds(0, MB2)], stage.at[j, pl.ds(MA2, MB2)], at, wait)
-
-        @pl.when(jnp.logical_not(moving))
-        def _():
-            own_piece(
-                w_in, w_out, rank, C1, C2,
-                lambda src: go(src, stage.at[j, pl.ds(0, C2)], at, wait),
-            )
-
-    def from_stayer(wait, j, moving, rank, p):
-        @pl.when(moving)
-        def _():
-            go(recv1.at[p, pl.ds(0, C2)], stage.at[j, pl.ds(0, C2)], sem.at[j // SIZE], wait)
-
-    def out(wait, g):
-        part = pl.ds(g * SIZE, SIZE)
-        go(stage.at[part], buf2.at[part], osem, wait)
-
-    for mine, visit in ((True, from_mover), (False, from_stayer)):
+    @pl.when(i_move)
+    def _():
+        def step(k, w, tile):
+            m = order[k]
+            t = order[k + N // 2]
+            at = sem.at[m // SIZE]
+            go(w.at[pl.ds(tile + C1, C2)], stage.at[t], sem.at[t // SIZE], False)
+            go(w.at[pl.ds(tile + NPART + C1, MA2)], stage.at[m, pl.ds(0, MA2)], at, False)
+            go(recv1.at[partner[m], pl.ds(0, MB2)], stage.at[m, pl.ds(MA2, MB2)], at, False)
+
+        both_halves(step, w_in, w_out)
+        for g in range(GROUPS):
+            settled(stage.at[group_of(g)], sem.at[g])
+            go(stage.at[group_of(g)], buf2.at[group_of(g)], osem, False)
+        settled(stage, osem)
+
+    @pl.when(jnp.logical_not(i_move))
+    def _():
+        forward(order, partner, stage, buf2, sem, osem, C2, ((recv1, 0, 0, C2),))
+
+
+def forward(order, partner, stage, buf, sem, osem, tiles, pieces, between=None):
+    groups = N // 2 // SIZE
+
+    def load(k):
+        m = order[k]
+        p = partner[m]
+        for array, lo, to, size in pieces:
+            go(array.at[p, pl.ds(lo, size)], stage.at[k, pl.ds(to, size)], sem.at[k // SIZE], False)
+
+    each_mover(load)
+    if between is not None:
+        between()
+    for g in range(groups):
+        settled(stage.at[group_of(g), pl.ds(0, tiles)], sem.at[g])
+
+        def send(i, c):
+            k = g * SIZE + i
+            go(stage.at[k, pl.ds(0, tiles)], buf.at[order[k], pl.ds(0, tiles)], osem, False)
+            return c
+
+        lax.fori_loop(0, SIZE, send, 0, unroll=UNROLL)
+    settled(stage.at[pl.ds(0, N // 2), pl.ds(0, tiles)], osem)
+
+
+def third_kernel(
+    me, partner, order, recv1, recv2, answers, buf3, stage, tok, sem, osem, tsem
+):
+    my = me[0]
+    i_move = partner[my] != my
+    go(answers, tok, tsem, False)
+
+    def tokens():
+        go(answers, tok, tsem, True)
+        go(tok, buf3.at[:, pl.ds(C3, TOK)], tsem, False)
+
+    for mine, early, late in ((True, MB2, MA2), (False, C2, C2)):
+        held = C1 - late
+
         @pl.when(i_move == mine)
         def _():
-            copies(partner, functools.partial(visit, False))
-            copies(partner, functools.partial(visit, True), functools.partial(out, False))
-            copies(partner, nothing, functools.partial(out, True))
-
-
-def third_kernel(me, partner, recv1, recv2, answers, buf3, stage, sem, osem):
-    my = me[0]
-    i_move = partner[my] != my
-
-    def visit(early, late, wait, j, moving, rank, p):
-        at = sem.at[j // SIZE]
-
-        @pl.when(moving)
-        def _():
-            go(recv1.at[p, pl.ds(early, C1 - late)], stage.at[j, pl.ds(0, C1 - late)], at, wait)
-            go(recv2.at[p, pl.ds(0, late)], stage.at[j, pl.ds(C1 - late, late)], at, wait)
-
-    def token(wait, g):
-        part = pl.ds(g * SIZE, SIZE)
-        go(answers.at[part], stage.at[part, pl.ds(C3, TOK)], sem.at[g], wait)
-
-    def out(wait, g):
-        part = pl.ds(g * SIZE, SIZE)
-        if not wait:
-            token(True, g)
-        go(stage.at[part], buf3.at[part], osem, wait)
-
-    for mine, early, late in ((True, MB2, MA2), (False, C2, C2)):
-        step = functools.partial(visit, early, late)
-
-        @pl.when(i_move == mine)
-        def _():
-            copies(partner, functools.partial(step, False), functools.partial(token, False))
-            copies(partner, functools.partial(step, True), functools.partial(out, False))
-            copies(partner, nothing, functools.partial(out, True))
+            forward(
+                order, partner, stage, buf3, sem, osem, C3,
+                ((recv1, early, 0, held), (recv2, 0, held, late)),
+                tokens,
+            )
+
+    go(tok, buf3.at[:, pl.ds(C3, TOK)], tsem, True)
 
 
 def settle_kernel(me, partner, w_in, w_out, recv2, new_in, new_out, stage, sem, osem):
@@ -290,31 +327,21 @@
 
 
 def last_kernel(
-    me, partner, recv3, pos, one, two, gate_one, gate_two, in_, out_,
-    res_one, res_two, new_in, new_out, stage, sem, osem,
+    me, partner, order, recv3, pos, one, two, gate_one, gate_two, in_, out_,
+    res_one, res_two, new_in, new_out, stage, tok, sem, osem, tsem,
 ):
     my = me[0]
     i_move = partner[my] != my
+    go(recv3.at[:, pl.ds(C3, TOK)], tok, tsem, False)
 
     def load(wait, g):
-        part = pl.ds(g * SIZE, SIZE)
-        go(recv3.at[part], stage.at[part], sem.at[g], wait)
-
-    def visit(wait, j, moving, rank, p):
-        offset = jnp.where(moving, NPART + MB2, C2)
-        own_piece(
-            new_in, new_out, rank, offset, C3,
-            lambda dst: go(stage.at[j, pl.ds(0, C3)], dst, osem, wait),
-        )
-
-    for g in range(GROUPS):
-        load(False, g)
-    for g in range(GROUPS):
-        load(True, g)
-
-    @pl.when(i_move)
-    def _():
-        copies(partner, functools.partial(visit, False))
+        part = group_of(g)
+        go(recv3.at[part, pl.ds(0, C3)], stage.at[part], sem.at[g], wait)
+
+    @pl.when(i_move)
+    def _():
+        for g in range(GROUPS):
+            load(False, g)
 
     rows = one.shape[0]
     width = one.shape[1]
@@ -324,7 +351,20 @@
     late = pos[:, 1:2]
     lane = lax.broadcasted_iota(jnp.int32, (total, N * 8), 1)
     hot = lambda where: (lane == where).astype(jnp.float32).astype(BF)
-    flat = lambda c: stage[:, C3 + c].astype(jnp.float32).reshape(N * 8, 128).astype(BF)
+
+    @pl.when(i_move)
+    def _():
+        for g in range(GROUPS):
+            load(True, g)
+
+        def step(k, w, tile):
+            go(stage.at[order[k + N // 2]], w.at[pl.ds(tile + C2, C3)], osem, False)
+            go(stage.at[order[k]], w.at[pl.ds(tile + NPART + MB2, C3)], osem, False)
+
+        both_halves(step, new_in, new_out)
+
+    go(recv3.at[:, pl.ds(C3, TOK)], tok, tsem, True)
+    flat = lambda c: tok[:, c].astype(jnp.float32).reshape(N * 8, 128).astype(BF)
     full = jnp.concatenate([flat(c) for c in range(cols)], axis=1)
     tail = jnp.concatenate([flat(cols + c) for c in range(cols // 2)], axis=1)
     top = jnp.dot(hot(early), full, preferred_element_type=jnp.float32)
@@ -344,7 +384,7 @@
 
     @pl.when(i_move)
     def _():
-        copies(partner, functools.partial(visit, True))
+        settled(stage, osem)
 
 
 def shape(*dims, dtype=BF):
@@ -368,27 +408,31 @@
     me = lax.axis_index(AXES).astype(jnp.int32).reshape(1)
     w_in = tiles_of(weight_in, width, ff)
     w_out = tiles_of(weight_out, ff, width)
-    buf1, pos = pl.pallas_call(
+    buf1, pos, order = pl.pallas_call(
         first_kernel,
-        out_shape=(shape(N, C1 + TOK, 8, 128), shape(2 * rows, 2, dtype=jnp.int32)),
+        out_shape=(
+            shape(N, C1 + TOK, 8, 128),
+            shape(2 * rows, 2, dtype=jnp.int32),
+            shape(N, dtype=jnp.int32),
+        ),
         in_specs=[SMEM, SMEM, HBM, HBM] + [VMEM] * 6,
-        out_specs=(HBM, VMEM),
+        out_specs=(HBM, VMEM, SMEM),
         scratch_shapes=[pltpu.VMEM((N, C1 + TOK, 8, 128), BF), SEMS, DMA],
         name="first",
     )(
         me, partner, w_in, w_out, group_one, group_two,
         routes_one.reshape(1, rows), routes_two.reshape(1, rows),
-        norm_gain.reshape(1, width), old_place.reshape(1, N),
+        norm_gain.reshape(width // 128, 128), old_place.reshape(1, N),
     )
     recv1 = exchange(buf1)
     buf2 = pl.pallas_call(
         second_kernel,
         out_shape=shape(N, C2, 8, 128),
-        in_specs=[SMEM, SMEM, HBM, HBM, HBM],
+        in_specs=[SMEM, SMEM, SMEM, HBM, HBM, HBM],
         out_specs=HBM,
         scratch_shapes=[pltpu.VMEM((N, C2, 8, 128), BF), SEMS, DMA],
         name="second",
-    )(me, partner, w_in, w_out, recv1)
+    )(me, partner, order, w_in, w_out, recv1)
     recv2 = exchange(buf2)
     arrived = recv1[:, C1:]
     cols = width // 128
@@ -407,11 +451,13 @@
     buf3 = pl.pallas_call(
         third_kernel,
         out_shape=shape(N, C3 + TOK, 8, 128),
-        in_specs=[SMEM, SMEM, HBM, HBM, pl.BlockSpec(memory_space=pl.ANY)],
+        in_specs=[SMEM, SMEM, SMEM, HBM, HBM, HBM],
         out_specs=HBM,
-        scratch_shapes=[pltpu.VMEM((N, C3 + TOK, 8, 128), BF), SEMS, DMA],
+        scratch_shapes=[
+            pltpu.VMEM((N // 2, C3, 8, 128), BF), pltpu.VMEM((N, TOK, 8, 128), BF), SEMS, DMA, DMA,
+        ],
         name="third",
-    )(me, partner, recv1, recv2, answers)
+    )(me, partner, order, recv1, recv2, answers)
     recv3 = exchange(buf3)
     new_in, new_out = pl.pallas_call(
         settle_kernel,
@@ -426,13 +472,15 @@
         out_shape=(
             shape(rows, width), shape(rows, width), shape(HALF, 8, 128), shape(HALF, 8, 128),
         ),
-        in_specs=[SMEM, SMEM, HBM] + [VMEM] * 5 + [HBM, HBM],
+        in_specs=[SMEM, SMEM, SMEM, HBM] + [VMEM] * 5 + [HBM, HBM],
         out_specs=(VMEM, VMEM, HBM, HBM),
-        scratch_shapes=[pltpu.VMEM((N, C3 + TOK, 8, 128), BF), SEMS, DMA],
-        input_output_aliases={8: 2, 9: 3},
+        scratch_shapes=[
+            pltpu.VMEM((N, C3, 8, 128), BF), pltpu.VMEM((N, TOK, 8, 128), BF), SEMS, DMA, DMA,
+        ],
+        input_output_aliases={9: 2, 10: 3},
         name="last",
     )(
-        me, partner, recv3, pos, group_one, group_two,
+        me, partner, order, recv3, pos, group_one, group_two,
         gates_one.reshape(rows, 1), gates_two.reshape(rows, 1), new_in, new_out,
     )
     return (res_one, res_two, array_of(new_in, width, ff), array_of(new_out, ff, width))

time: 323 us -> 316 us (0.978)
  Pallas kernels: 39.4 us -> 28.1 us
    pallas_call x1, Pallas kernels: 10.3 us -> 5.45 us  [local(): pl.pallas_call(last_kernel, out_shape=(shape(rows, width), shape(rows, wi...]
    pallas_call x1, Pallas kernels: 9.98 us -> 6.37 us  [local(): pl.pallas_call(first_kernel, out_shape=(shape(N, C1 + TOK, 8, 128), shape...]
    pallas_call x1, Pallas kernels: 6.77 us -> 3.39 us  [local(): pl.pallas_call(second_kernel, out_shape=shape(N, C2, 8, 128), in_specs=[S...]
  transfers between devices with their start and end apart: 2 -> 2, of which waited for: 2 -> 2; matrix products, arithmetic and copies ran while one was open for 9% -> 9% of each run, Pallas kernels for 2% -> 3%
where the time goes in v3:
time: 316 us; the launch traced here: 314 us
  waiting for transfers between devices  129 us (41%)
  blocking collectives  108 us (34%)
  Pallas kernels  28.1 us (9%)
  matrix products  20.5 us (6%)
  starting transfers between devices  18.1 us (6%)
  local copies, waits for them, and re-layouts  7.36 us (2%)
    all_to_all x2, waiting for transfers between devices, exchange(): return lax.all_to_all(x, AXES, split_axis=0, concat_axis=0, tiled=True)  129 us
    all_to_all x1, blocking collectives, exchange(): return lax.all_to_all(x, AXES, split_axis=0, concat_axis=0, tiled=True)  108 us
    dot_general x1, matrix products, local(): jnp.dot(hidden, weight_out[0], preferred_element_type=jnp.float32)  20.5 us
    all_to_all x2, starting transfers between devices, exchange(): return lax.all_to_all(x, AXES, split_axis=0, concat_axis=0, tiled=True)  18.1 us
    pallas_call x1, Pallas kernels, local(): pl.pallas_call(settle_kernel, out_shape=(shape(HALF, 8, 128), shape(HALF,...  8.09 us
    pallas_call x1, Pallas kernels, local(): pl.pallas_call(first_kernel, out_shape=(shape(N, C1 + TOK, 8, 128), shape...  6.37 us
  transfers between devices with their start and end apart: 2, of which 2 were waited for; matrix products, arithmetic and copies ran while one was open for 9% of the time, Pallas kernels for 3%

profile of v3, /device:TPU:37, one launch (start us, length us, event | category | flops | bytes accessed | tf_op | source)
XLA Modules:
  0.0 313.5 jit_solution(15535225735230310868)
XLA Ops:
  0.6 6.4 %first.1 = (bf16[128,30,8,128]{3,2,1,0:T(8,128)(2,1)}, s32[384,2]{1,0:T(8,128)}, s32[128]{0:T(128)}) custom-call(s32[1]{0:T(128)} %bitcast.me, s32[128]{0:T(128)} %partner.9, bf16[2304,8,128]{2,1,0:T(8,128)(2,1)} %bitcast.55, bf16[2304,8,128]{2,1,0:T(8,128)(2,1)} %bitcast.58, bf16[192,768]{1,0:T(8,128)(2,1)} %one.3, bf16[192,768]{1,0:T(8,128)(2,1)} %two.3, ...), custom_call_target="tpu_custom_call" | custom-call | tf_op jit(solution)/shard_map/first/pallas_call | solution.py:411
  7.0 107.9 %all_to_all.15.recv1 = bf16[128,30,8,128]{3,2,1,0:T(8,128)(2,1)} all-to-all(bf16[128,30,8,128]{3,2,1,0:T(8,128)(2,1)} %get-tuple-element.14), channel_id=1, replica_groups=mesh['gx'=8,'gy'=16] {'gx','gy'}, dimensions={0} | all-to-all | bytes 15728640 | tf_op jit(solution)/shard_map/all_to_all | solution.py:395
  114.9 3.4 %second.1 = bf16[128,20,8,128]{3,2,1,0:T(8,128)(2,1)} custom-call(s32[1]{0:T(128)} %bitcast.me, s32[128]{0:T(128)} %partner.9, s32[128]{0:T(128)} %get-tuple-element.13.order, bf16[2304,8,128]{2,1,0:T(8,128)(2,1)} %bitcast.56, bf16[2304,8,128]{2,1,0:T(8,128)(2,1)} %bitcast.59, bf16[128,30,8,128]{3,2,1,0:T(8,128)(2,1)} %all_to_all.15.recv1), custom_call_target="tpu_custom_call" | custom-call | tf_op jit(solution)/shard_map/second/pallas_call | solution.py:428
  118.3 0.0 slice-start
  118.3 9.7 %all-to-all-start.1 = ((bf16[128,20,8,128]{3,2,1,0:T(8,128)(2,1)}), bf16[128,20,8,128]{3,2,1,0:T(8,128)(2,1)}, u32[]{:S(2)}, u32[]{:S(2)}) async-start(bf16[128,20,8,128]{3,2,1,0:T(8,128)(2,1)} %second.1), calls=%async_computation.1 | async-start | bytes 10485760 | tf_op jit(solution)/shard_map/all_to_all | solution.py:395
  128.0 0.6 copy.23
  128.6 0.4 reshape.85
  129.0 1.5 slice_bitcast_fusion.1
  130.5 20.5 %fusion.4 = bf16[1536,768]{1,0:T(8,128)(2,1)} fusion(bf16[1,3072,768]{2,1,0:T(8,128)(2,1)} %param.19, bf16[1,768,3072]{2,1,0:T(8,128)(2,1)} %param.18, bf16[512,768]{1,0:T(8,128)(2,1)S(1)} %reshape.85, bf16[1024,768]{1,0:T(8,128)(2,1)S(1)} %slice_bitcast_fusion.1), kind=kOutput, calls=%fused_computation.4 | convolution fusion | flops 14510850048 | bytes 14155776 | tf_op jit(solution)/shard_map/dot_general | solution.py:446
  151.0 1.2 slice.22
  152.2 0.2 reshape.87
  152.4 0.4 copy.19
  152.8 1.5 slice_bitcast_fusion
  154.3 1.6 pad_maximum_fusion.answers
  155.9 35.2 %all-to-all-done.1.recv2 = bf16[128,20,8,128]{3,2,1,0:T(8,128)(2,1)} async-done(((bf16[128,20,8,128]{3,2,1,0:T(8,128)(2,1)}), bf16[128,20,8,128]{3,2,1,0:T(8,128)(2,1)}, u32[]{:S(2)}, u32[]{:S(2)}) %all-to-all-start.1) | async-done | bytes 5242912 | tf_op jit(solution)/shard_map/all_to_all | solution.py:395
  191.1 4.7 %third.1 = bf16[128,30,8,128]{3,2,1,0:T(8,128)(2,1)} custom-call(s32[1]{0:T(128)} %bitcast.me, s32[128]{0:T(128)} %partner.9, s32[128]{0:T(128)} %get-tuple-element.13.order, bf16[128,30,8,128]{3,2,1,0:T(8,128)(2,1)} %all_to_all.15.recv1, bf16[128,20,8,128]{3,2,1,0:T(8,128)(2,1)} %all-to-all-done.1.recv2, bf16[128,9,8,128]{3,2,1,0:T(8,128)(2,1)} %pad_maximum_fusion.answers), custom_call_target="tpu_custom_call" | custom-call | tf_op jit(solution)/shard_map/third/pallas_call | solution.py:451
  195.9 0.0 copy-start
  195.9 0.0 copy-start.1
  195.9 8.5 %all-to-all-start.2 = ((bf16[128,30,8,128]{3,2,1,0:T(8,128)(2,1)}), bf16[128,30,8,128]{3,2,1,0:T(8,128)(2,1)}, u32[]{:S(2)}, u32[]{:S(2)}) async-start(bf16[128,30,8,128]{3,2,1,0:T(8,128)(2,1)} %third.1), calls=%async_computation.2 | async-start | bytes 15728640 | tf_op jit(solution)/shard_map/all_to_all | solution.py:395
  204.4 0.8 copy.20.gate_one
  205.1 0.8 copy.21.gate_two
  205.9 8.1 %settle.1 = (bf16[2304,8,128]{2,1,0:T(8,128)(2,1)}, bf16[2304,8,128]{2,1,0:T(8,128)(2,1)}) custom-call(s32[1]{0:T(128)} %bitcast.me, s32[128]{0:T(128)} %partner.9, bf16[2304,8,128]{2,1,0:T(8,128)(2,1)} %bitcast.57, bf16[2304,8,128]{2,1,0:T(8,128)(2,1)} %bitcast.60, bf16[2560,8,128]{2,1,0:T(8,128)(2,1)} %bitcast.27.recv2), custom_call_target="tpu_custom_call" | custom-call | tf_op jit(solution)/shard_map/settle/pallas_call | solution.py:462
  214.0 93.9 %all-to-all-done.2.recv3 = bf16[128,30,8,128]{3,2,1,0:T(8,128)(2,1)} async-done(((bf16[128,30,8,128]{3,2,1,0:T(8,128)(2,1)}), bf16[128,30,8,128]{3,2,1,0:T(8,128)(2,1)}, u32[]{:S(2)}, u32[]{:S(2)}) %all-to-all-start.2) | async-done | bytes 7864352 | tf_op jit(solution)/shard_map/all_to_all | solution.py:395
  307.9 5.5 %last.1 = (bf16[192,768]{1,0:T(8,128)(2,1)}, bf16[192,768]{1,0:T(8,128)(2,1)}, bf16[2304,8,128]{2,1,0:T(8,128)(2,1)}, bf16[2304,8,128]{2,1,0:T(8,128)(2,1)}) custom-call(s32[1]{0:T(128)} %bitcast.me, s32[128]{0:T(128)} %partner.9, s32[128]{0:T(128)} %get-tuple-element.13.order, ...), custom_call_target="tpu_custom_call", output_to_operand_aliasing={{2}: (9, {}), {3}: (10, {})} | custom-call | tf_op jit(solution)/shard_map/last/pallas_call | solution.py:470
  (3 shorter events, 0.0 us)
Async XLA Ops:
  118.3 9.7 %slice-start = ((bf16[128,30,8,128]{3,2,1,0:T(8,128)(2,1)}), bf16[128,3,8,128]{3,2,1,0:T(8,128)(2,1)S(1)}, s32[]{:S(2)}) async-start(bf16[128,30,8,128]{3,2,1,0:T(8,128)(2,1)} %all_to_all.15.recv1), calls=%async_computation.3 | async-start | bytes 1572864 | tf_op jit(solution)/shard_map/slice | solution.py:440
  118.3 72.8 %all-to-all-start.1 = ((bf16[128,20,8,128]{3,2,1,0:T(8,128)(2,1)}), bf16[128,20,8,128]{3,2,1,0:T(8,128)(2,1)}, u32[]{:S(2)}, u32[]{:S(2)}) async-start(bf16[128,20,8,128]{3,2,1,0:T(8,128)(2,1)} %second.1), calls=%async_computation.1 | async-start | bytes 10485760 | tf_op jit(solution)/shard_map/all_to_all | solution.py:395
  195.9 8.5 %copy-start = (f32[192]{0:T(256)S(1)}, f32[192]{0:T(256)}, u32[]{:S(2)}) copy-start(f32[192]{0:T(256)} %param.13) | copy-start | bytes 2308
  195.9 9.3 %copy-start.1 = (f32[192]{0:T(256)S(1)}, f32[192]{0:T(256)}, u32[]{:S(2)}) copy-start(f32[192]{0:T(256)} %param.16) | copy-start | bytes 2308
  195.9 112.0 %all-to-all-start.2 = ((bf16[128,30,8,128]{3,2,1,0:T(8,128)(2,1)}), bf16[128,30,8,128]{3,2,1,0:T(8,128)(2,1)}, u32[]{:S(2)}, u32[]{:S(2)}) async-start(bf16[128,30,8,128]{3,2,1,0:T(8,128)(2,1)} %third.1), calls=%async_computation.2 | async-start | bytes 15728640 | tf_op jit(solution)/shard_map/all_to_all | solution.py:395

commit v4 on v3

--- a/solution.py
+++ b/solution.py
@@ -103,11 +103,14 @@
 
 
 def first_kernel(
-    me, partner, w_in, w_out, one, two, routes_one, routes_two, gain, place,
-    buf1, pos, order, stage, sem, osem,
+    me, partner, w_in, w_out, *refs,
 ):
+    given, (buf1, pos_out, order, stage, *held, pos, sem, osem, isem) = refs[:6], refs[6:]
+    one, two, routes_one, routes_two, gain, place = held
     my = me[0]
     i_move = partner[my] != my
+    for src, dst in zip(given, held):
+        go(src, dst, isem, False)
 
     def sort(j, counts):
         movers, stayers = counts
@@ -132,6 +135,8 @@
     width = one.shape[1]
     cols = width // 128
     total = 2 * rows
+    for src, dst in zip(given, held):
+        go(src, dst, isem, True)
     slots = place[...]
     lower = (
         lax.broadcasted_iota(jnp.int32, (rows, rows), 1)
@@ -158,6 +163,7 @@
     late = jnp.where(place_in < 8, -1, target * 8 + place_in - 8)
     pos[:, 0:1] = early
     pos[:, 1:2] = late
+    go(pos, pos_out, isem, False)
 
     def tiles(lo, size):
         go(stage.at[:, pl.ds(lo, size)], buf1.at[:, pl.ds(lo, size)], osem, False)
@@ -191,6 +197,7 @@
     for c in range(cols):
         stage[:, C1 + c] = cut(top, c).astype(BF)
     tiles(C1, cols)
+    go(pos, pos_out, isem, True)
     settled(stage.at[:, pl.ds(C1, TOK)], osem)
 
     @pl.when(i_move)
@@ -198,78 +205,76 @@
         settled(stage.at[:, pl.ds(0, C1)], osem)
 
 
-def second_kernel(me, partner, order, w_in, w_out, recv1, buf2, stage, sem, osem):
+def second_own_kernel(me, partner, order, w_in, w_out, buf2, stage, sem, osem):
     my = me[0]
-    i_move = partner[my] != my
-
-    @pl.when(i_move)
+
+    @pl.when(partner[my] != my)
     def _():
         def step(k, w, tile):
             m = order[k]
             t = order[k + N // 2]
-            at = sem.at[m // SIZE]
-            go(w.at[pl.ds(tile + C1, C2)], stage.at[t], sem.at[t // SIZE], False)
-            go(w.at[pl.ds(tile + NPART + C1, MA2)], stage.at[m, pl.ds(0, MA2)], at, False)
-            go(recv1.at[partner[m], pl.ds(0, MB2)], stage.at[m, pl.ds(MA2, MB2)], at, False)
+            at = sem.at[k // SIZE]
+            go(w.at[pl.ds(tile + C1, C2)], stage.at[k, pl.ds(0, C2)], at, False)
+            go(w.at[pl.ds(tile + NPART + C1, MA2)], stage.at[k, pl.ds(C2, MA2)], at, False)
 
         both_halves(step, w_in, w_out)
-        for g in range(GROUPS):
+        for g in range(N // 2 // SIZE):
             settled(stage.at[group_of(g)], sem.at[g])
-            go(stage.at[group_of(g)], buf2.at[group_of(g)], osem, False)
+
+            def send(i, c):
+                k = g * SIZE + i
+                m = order[k]
+                t = order[k + N // 2]
+                go(stage.at[k, pl.ds(0, C2)], buf2.at[t], osem, False)
+                go(stage.at[k, pl.ds(C2, MA2)], buf2.at[m, pl.ds(0, MA2)], osem, False)
+                return c
+
+            lax.fori_loop(0, SIZE, send, 0, unroll=UNROLL)
         settled(stage, osem)
 
-    @pl.when(jnp.logical_not(i_move))
-    def _():
-        forward(order, partner, stage, buf2, sem, osem, C2, ((recv1, 0, 0, C2),))
-
-
-def forward(order, partner, stage, buf, sem, osem, tiles, pieces, between=None):
+
+def forward_kernel(of_mover, of_stayer, tokens, me, partner, order, recv, *refs):
+    my = me[0]
+    i_move = partner[my] != my
+    if tokens:
+        answers, buf, stage, tok, sem, osem, tsem = refs
+        go(answers, tok, tsem, False)
+    else:
+        _, buf, stage, sem, osem = refs
+
+    def between():
+        if tokens:
+            go(answers, tok, tsem, True)
+            go(tok, buf.at[:, pl.ds(C3, TOK)], tsem, False)
+
+    for mine, piece in ((True, of_mover), (False, of_stayer)):
+        @pl.when(i_move == mine)
+        def _():
+            forward(order, partner, stage, buf, sem, osem, recv, *piece, between)
+
+    if tokens:
+        go(tok, buf.at[:, pl.ds(C3, TOK)], tsem, True)
+
+
+def forward(order, partner, stage, buf, sem, osem, recv, lo, to, size, between):
     groups = N // 2 // SIZE
 
     def load(k):
-        m = order[k]
-        p = partner[m]
-        for array, lo, to, size in pieces:
-            go(array.at[p, pl.ds(lo, size)], stage.at[k, pl.ds(to, size)], sem.at[k // SIZE], False)
+        p = partner[order[k]]
+        go(recv.at[p, pl.ds(lo, size)], stage.at[k, pl.ds(0, size)], sem.at[k // SIZE], False)
 
     each_mover(load)
-    if between is not None:
-        between()
+    between()
     for g in range(groups):
-        settled(stage.at[group_of(g), pl.ds(0, tiles)], sem.at[g])
+        settled(stage.at[group_of(g), pl.ds(0, size)], sem.at[g])
 
         def send(i, c):
             k = g * SIZE + i
-            go(stage.at[k, pl.ds(0, tiles)], buf.at[order[k], pl.ds(0, tiles)], osem, False)
+            go(stage.at[k, pl.ds(0, size)], buf.at[order[k], pl.ds(to, size)], osem, False)
             return c
 
         lax.fori_loop(0, SIZE, send, 0, unroll=UNROLL)
-    settled(stage.at[pl.ds(0, N // 2), pl.ds(0, tiles)], osem)
-
-
-def third_kernel(
-    me, partner, order, recv1, recv2, answers, buf3, stage, tok, sem, osem, tsem
-):
-    my = me[0]
-    i_move = partner[my] != my
-    go(answers, tok, tsem, False)
-
-    def tokens():
-        go(answers, tok, tsem, True)
-        go(tok, buf3.at[:, pl.ds(C3, TOK)], tsem, False)
-
-    for mine, early, late in ((True, MB2, MA2), (False, C2, C2)):
-        held = C1 - late
-
-        @pl.when(i_move == mine)
-        def _():
-            forward(
-                order, partner, stage, buf3, sem, osem, C3,
-                ((recv1, early, 0, held), (recv2, 0, held, late)),
-                tokens,
-            )
-
-    go(tok, buf3.at[:, pl.ds(C3, TOK)], tsem, True)
+    settled(stage.at[pl.ds(0, N // 2), pl.ds(0, size)], osem)
 
 
 def settle_kernel(me, partner, w_in, w_out, recv2, new_in, new_out, stage, sem, osem):
@@ -327,9 +332,11 @@
 
 
 def last_kernel(
-    me, partner, order, recv3, pos, one, two, gate_one, gate_two, in_, out_,
-    res_one, res_two, new_in, new_out, stage, tok, sem, osem, tsem,
+    me, partner, order, recv3, *refs,
 ):
+    given, (in_, out_, *results, new_in, new_out) = refs[:5], refs[5:11]
+    stage, tok, *held, res_one, res_two, sem, osem, tsem, isem = refs[11:]
+    pos, one, two, gate_one, gate_two = held
     my = me[0]
     i_move = partner[my] != my
     go(recv3.at[:, pl.ds(C3, TOK)], tok, tsem, False)
@@ -343,10 +350,14 @@
         for g in range(GROUPS):
             load(False, g)
 
+    for src, dst in zip(given, held):
+        go(src, dst, isem, False)
     rows = one.shape[0]
     width = one.shape[1]
     cols = width // 128
     total = 2 * rows
+    for src, dst in zip(given, held):
+        go(src, dst, isem, True)
     early = pos[:, 0:1]
     late = pos[:, 1:2]
     lane = lax.broadcasted_iota(jnp.int32, (total, N * 8), 1)
@@ -381,6 +392,9 @@
             h = slice(c // 2 * 128, (c // 2 + 1) * 128)
             answer = top[r, s] + (odd if c % 2 else even)[r, h]
             res[:, s] = (group[:, s].astype(jnp.float32) + gate[...] * answer).astype(BF)
+        go(res, results[b], isem, False)
+    for b, res in enumerate((res_one, res_two)):
+        go(res, results[b], isem, True)
 
     @pl.when(i_move)
     def _():
@@ -415,9 +429,15 @@
             shape(2 * rows, 2, dtype=jnp.int32),
             shape(N, dtype=jnp.int32),
         ),
-        in_specs=[SMEM, SMEM, HBM, HBM] + [VMEM] * 6,
-        out_specs=(HBM, VMEM, SMEM),
-        scratch_shapes=[pltpu.VMEM((N, C1 + TOK, 8, 128), BF), SEMS, DMA],
+        in_specs=[SMEM, SMEM, HBM, HBM] + [HBM] * 6,
+        out_specs=(HBM, HBM, SMEM),
+        scratch_shapes=[
+            pltpu.VMEM((N, C1 + TOK, 8, 128), BF),
+            pltpu.VMEM((rows, width), BF), pltpu.VMEM((rows, width), BF),
+            pltpu.VMEM((1, rows), jnp.int32), pltpu.VMEM((1, rows), jnp.int32),
+            pltpu.VMEM((width // 128, 128), jnp.float32), pltpu.VMEM((1, N), jnp.int32),
+            pltpu.VMEM((2 * rows, 2), jnp.int32), SEMS, DMA, DMA,
+        ],
         name="first",
     )(
         me, partner, w_in, w_out, group_one, group_two,
@@ -426,13 +446,22 @@
     )
     recv1 = exchange(buf1)
     buf2 = pl.pallas_call(
-        second_kernel,
+        second_own_kernel,
         out_shape=shape(N, C2, 8, 128),
-        in_specs=[SMEM, SMEM, SMEM, HBM, HBM, HBM],
+        in_specs=[SMEM, SMEM, SMEM, HBM, HBM],
         out_specs=HBM,
-        scratch_shapes=[pltpu.VMEM((N, C2, 8, 128), BF), SEMS, DMA],
-        name="second",
-    )(me, partner, order, w_in, w_out, recv1)
+        scratch_shapes=[pltpu.VMEM((N // 2, C2 + MA2, 8, 128), BF), SEMS, DMA],
+        name="second_own",
+    )(me, partner, order, w_in, w_out)
+    buf2 = pl.pallas_call(
+        functools.partial(forward_kernel, (0, MA2, MB2), (0, 0, C2), False),
+        out_shape=shape(N, C2, 8, 128),
+        in_specs=[SMEM, SMEM, SMEM, HBM, HBM],
+        out_specs=HBM,
+        scratch_shapes=[pltpu.VMEM((N // 2, C2, 8, 128), BF), SEMS, DMA],
+        input_output_aliases={4: 0},
+        name="second_forward",
+    )(me, partner, order, recv1, buf2)
     recv2 = exchange(buf2)
     arrived = recv1[:, C1:]
     cols = width // 128
@@ -449,15 +478,25 @@
     rest = rest.transpose(0, 2, 3, 1, 4).reshape(N, cols // 2, 8, 128)
     answers = jnp.concatenate([top, rest], axis=1)
     buf3 = pl.pallas_call(
-        third_kernel,
+        functools.partial(forward_kernel, (MB2, 0, C1 - MB2), (C2, 0, C1 - C2), True),
         out_shape=shape(N, C3 + TOK, 8, 128),
-        in_specs=[SMEM, SMEM, SMEM, HBM, HBM, HBM],
+        in_specs=[SMEM, SMEM, SMEM, HBM, HBM],
         out_specs=HBM,
         scratch_shapes=[
-            pltpu.VMEM((N // 2, C3, 8, 128), BF), pltpu.VMEM((N, TOK, 8, 128), BF), SEMS, DMA, DMA,
+            pltpu.VMEM((N // 2, C1 - MB2, 8, 128), BF), pltpu.VMEM((N, TOK, 8, 128), BF),
+            SEMS, DMA, DMA,
         ],
-        name="third",
-    )(me, partner, order, recv1, recv2, answers)
+        name="third_held",
+    )(me, partner, order, recv1, answers)
+    buf3 = pl.pallas_call(
+        functools.partial(forward_kernel, (0, C1 - MB2, MA2), (0, C1 - C2, C2), False),
+        out_shape=shape(N, C3 + TOK, 8, 128),
+        in_specs=[SMEM, SMEM, SMEM, HBM, HBM],
+        out_specs=HBM,
+        scratch_shapes=[pltpu.VMEM((N // 2, C2, 8, 128), BF), SEMS, DMA],
+        input_output_aliases={4: 0},
+        name="third_forward",
+    )(me, partner, order, recv2, buf3)
     recv3 = exchange(buf3)
     new_in, new_out = pl.pallas_call(
         settle_kernel,
@@ -472,10 +511,15 @@
         out_shape=(
             shape(rows, width), shape(rows, width), shape(HALF, 8, 128), shape(HALF, 8, 128),
         ),
-        in_specs=[SMEM, SMEM, SMEM, HBM] + [VMEM] * 5 + [HBM, HBM],
-        out_specs=(VMEM, VMEM, HBM, HBM),
+        in_specs=[SMEM, SMEM, SMEM, HBM] + [HBM] * 7,
+        out_specs=(HBM, HBM, HBM, HBM),
         scratch_shapes=[
-            pltpu.VMEM((N, C3, 8, 128), BF), pltpu.VMEM((N, TOK, 8, 128), BF), SEMS, DMA, DMA,
+            pltpu.VMEM((N, C3, 8, 128), BF), pltpu.VMEM((N, TOK, 8, 128), BF),
+            pltpu.VMEM((2 * rows, 2), jnp.int32),
+            pltpu.VMEM((rows, width), BF), pltpu.VMEM((rows, width), BF),
+            pltpu.VMEM((rows, 1), jnp.float32), pltpu.VMEM((rows, 1), jnp.float32),
+            pltpu.VMEM((rows, width), BF), pltpu.VMEM((rows, width), BF),
+            SEMS, DMA, DMA, DMA,
         ],
         input_output_aliases={9: 2, 10: 3},
         name="last",

time: 316 us -> 321 us (1.016)
  blocking collectives: 108 us -> 0 us
  waiting for transfers between devices: 129 us -> 225 us
  starting transfers between devices: 18.1 us -> 28 us
  Pallas kernels: 28.1 us -> 35.6 us
    all_to_all x1 -> x0, blocking collectives: 108 us -> none  [exchange(): return lax.all_to_all(x, AXES, split_axis=0, concat_axis=0, tiled=True)]
    all_to_all x2 -> x3, waiting for transfers between devices: 129 us -> 225 us  [exchange(): return lax.all_to_all(x, AXES, split_axis=0, concat_axis=0, tiled=True)]
    all_to_all x2 -> x3, starting transfers between devices: 18.1 us -> 28 us  [exchange(): return lax.all_to_all(x, AXES, split_axis=0, concat_axis=0, tiled=True)]
    pallas_call x2 -> x4, Pallas kernels: 8.14 us -> 14.3 us  [the longest x1 4.38 us: local(): pl.pallas_call(functools.partial(forward_kernel, (MB2, 0, C1 - MB2), (C2,...]
  transfers between devices with their start and end apart: 2 -> 3, of which waited for: 2 -> 3; matrix products, arithmetic and copies ran while one was open for 9% -> 10% of each run, Pallas kernels for 3% -> 5%
where the time goes in v4:
time: 321 us; the launch traced here: 320 us
  waiting for transfers between devices  225 us (70%)
  Pallas kernels  35.6 us (11%)
  starting transfers between devices  28 us (9%)
  matrix products  20.4 us (6%)
  local copies, waits for them, and re-layouts  8.57 us (3%)
    all_to_all x3, waiting for transfers between devices, exchange(): return lax.all_to_all(x, AXES, split_axis=0, concat_axis=0, tiled=True)  225 us
    all_to_all x3, starting transfers between devices, exchange(): return lax.all_to_all(x, AXES, split_axis=0, concat_axis=0, tiled=True)  28 us
    dot_general x1, matrix products, local(): jnp.dot(hidden, weight_out[0], preferred_element_type=jnp.float32)  20.4 us
    pallas_call x1, Pallas kernels, local(): pl.pallas_call(first_kernel, out_shape=(shape(N, C1 + TOK, 8, 128), shape...  7.85 us
    pallas_call x1, Pallas kernels, local(): pl.pallas_call(last_kernel, out_shape=(shape(rows, width), shape(rows, wi...  7.02 us
    pallas_call x1, Pallas kernels, local(): pl.pallas_call(settle_kernel, out_shape=(shape(HALF, 8, 128), shape(HALF,...  6.47 us
  transfers between devices with their start and end apart: 3, of which 3 were waited for; matrix products, arithmetic and copies ran while one was open for 10% of the time, Pallas kernels for 5%

profile of v4, /device:TPU:37, one launch (start us, length us, event | category | flops | bytes accessed | tf_op | source)
XLA Modules:
  0.0 319.8 jit_solution(4675579582504367450)
XLA Ops:
  0.6 7.8 %first.1 = (bf16[128,30,8,128]{3,2,1,0:T(8,128)(2,1)}, s32[384,2]{1,0:T(8,128)}, s32[128]{0:T(128)}) custom-call(s32[1]{0:T(128)} %bitcast.me, s32[128]{0:T(128)} %partner.13, bf16[2304,8,128]{2,1,0:T(8,128)(2,1)} %bitcast.54, bf16[2304,8,128]{2,1,0:T(8,128)(2,1)} %bitcast.57, bf16[192,768]{1,0:T(8,128)(2,1)} %refs_1_.3, bf16[192,768]{1,0:T(8,128)(2,1)} %refs_2_.1, ...), custom_call_target="tpu_custom_call" | custom-call | tf_op jit(solution)/shard_map/first/pallas_call | solution.py:425
  8.5 10.5 %all-to-all-start = ((bf16[128,30,8,128]{3,2,1,0:T(8,128)(2,1)}), bf16[128,30,8,128]{3,2,1,0:T(8,128)(2,1)}, u32[]{:S(2)}, u32[]{:S(2)}) async-start(bf16[128,30,8,128]{3,2,1,0:T(8,128)(2,1)} %get-tuple-element.14), calls=%async_computation | async-start | bytes 15728640 | tf_op jit(solution)/shard_map/all_to_all | solution.py:409
  19.0 4.1 %second_own.1.refs_0_ = bf16[128,20,8,128]{3,2,1,0:T(8,128)(2,1)} custom-call(s32[1]{0:T(128)} %bitcast.me, s32[128]{0:T(128)} %partner.13, s32[128]{0:T(128)} %get-tuple-element.13.order, bf16[2304,8,128]{2,1,0:T(8,128)(2,1)} %bitcast.55, bf16[2304,8,128]{2,1,0:T(8,128)(2,1)} %bitcast.58), custom_call_target="tpu_custom_call" | custom-call | tf_op jit(solution)/shard_map/second_own/pallas_call | solution.py:448
  23.1 99.5 %all-to-all-done.recv = bf16[128,30,8,128]{3,2,1,0:T(8,128)(2,1)} async-done(((bf16[128,30,8,128]{3,2,1,0:T(8,128)(2,1)}), bf16[128,30,8,128]{3,2,1,0:T(8,128)(2,1)}, u32[]{:S(2)}, u32[]{:S(2)}) %all-to-all-start) | async-done | bytes 7864352 | tf_op jit(solution)/shard_map/all_to_all | solution.py:409
  122.5 2.9 second_forward.1
  125.4 8.6 %all-to-all-start.1 = ((bf16[128,20,8,128]{3,2,1,0:T(8,128)(2,1)}), bf16[128,20,8,128]{3,2,1,0:T(8,128)(2,1)}, u32[]{:S(2)}, u32[]{:S(2)}) async-start(bf16[128,20,8,128]{3,2,1,0:T(8,128)(2,1)} %second_forward.1), calls=%async_computation.1 | async-start | bytes 10485760 | tf_op jit(solution)/shard_map/all_to_all | solution.py:409
  134.0 1.2 slice.20
  135.2 0.6 copy.25
  135.9 0.4 reshape.85
  136.2 1.5 slice_bitcast_fusion.1
  137.8 20.4 %fusion.4 = bf16[1536,768]{1,0:T(8,128)(2,1)} fusion(bf16[1,3072,768]{2,1,0:T(8,128)(2,1)} %param.19, bf16[1,768,3072]{2,1,0:T(8,128)(2,1)} %param.18, bf16[512,768]{1,0:T(8,128)(2,1)S(1)} %reshape.85, bf16[1024,768]{1,0:T(8,128)(2,1)S(1)} %slice_bitcast_fusion.1), kind=kOutput, calls=%fused_computation.4 | convolution fusion | flops 14510850048 | bytes 14155776 | tf_op jit(solution)/shard_map/dot_general | solution.py:475
  158.2 1.2 slice.22
  159.6 0.4 copy.21
  160.0 1.5 slice_bitcast_fusion
  161.5 1.6 pad_maximum_fusion.refs_0_
  163.1 4.4 %third_held.1.refs_0_ = bf16[128,30,8,128]{3,2,1,0:T(8,128)(2,1)} custom-call(s32[1]{0:T(128)} %bitcast.me, s32[128]{0:T(128)} %partner.13, s32[128]{0:T(128)} %get-tuple-element.13.order, bf16[128,30,8,128]{3,2,1,0:T(8,128)(2,1)} %all-to-all-done.recv, bf16[128,9,8,128]{3,2,1,0:T(8,128)(2,1)} %pad_maximum_fusion.refs_0_), custom_call_target="tpu_custom_call" | custom-call | tf_op jit(solution)/shard_map/third_held/pallas_call | solution.py:480
  167.5 29.6 %all-to-all-done.1.recv = bf16[128,20,8,128]{3,2,1,0:T(8,128)(2,1)} async-done(((bf16[128,20,8,128]{3,2,1,0:T(8,128)(2,1)}), bf16[128,20,8,128]{3,2,1,0:T(8,128)(2,1)}, u32[]{:S(2)}, u32[]{:S(2)}) %all-to-all-start.1) | async-done | bytes 5242912 | tf_op jit(solution)/shard_map/all_to_all | solution.py:409
  197.1 2.9 third_forward.1
  200.1 9.0 %all-to-all-start.2 = ((bf16[128,30,8,128]{3,2,1,0:T(8,128)(2,1)}), bf16[128,30,8,128]{3,2,1,0:T(8,128)(2,1)}, u32[]{:S(2)}, u32[]{:S(2)}) async-start(bf16[128,30,8,128]{3,2,1,0:T(8,128)(2,1)} %third_forward.1), calls=%async_computation.2 | async-start | bytes 15728640 | tf_op jit(solution)/shard_map/all_to_all | solution.py:409
  209.1 0.8 copy.22.refs_3_
  209.8 0.8 copy.23.refs_4_
  210.6 6.5 %settle.1 = (bf16[2304,8,128]{2,1,0:T(8,128)(2,1)}, bf16[2304,8,128]{2,1,0:T(8,128)(2,1)}) custom-call(s32[1]{0:T(128)} %bitcast.me, s32[128]{0:T(128)} %partner.13, bf16[2304,8,128]{2,1,0:T(8,128)(2,1)} %bitcast.56, bf16[2304,8,128]{2,1,0:T(8,128)(2,1)} %bitcast.59, bf16[2560,8,128]{2,1,0:T(8,128)(2,1)} %bitcast.27.recv2), custom_call_target="tpu_custom_call" | custom-call | tf_op jit(solution)/shard_map/settle/pallas_call | solution.py:501
  217.1 95.5 %all-to-all-done.2.recv3 = bf16[128,30,8,128]{3,2,1,0:T(8,128)(2,1)} async-done(((bf16[128,30,8,128]{3,2,1,0:T(8,128)(2,1)}), bf16[128,30,8,128]{3,2,1,0:T(8,128)(2,1)}, u32[]{:S(2)}, u32[]{:S(2)}) %all-to-all-start.2) | async-done | bytes 7864352 | tf_op jit(solution)/shard_map/all_to_all | solution.py:409
  312.6 7.0 %last.1 = (bf16[192,768]{1,0:T(8,128)(2,1)}, bf16[192,768]{1,0:T(8,128)(2,1)}, bf16[2304,8,128]{2,1,0:T(8,128)(2,1)}, bf16[2304,8,128]{2,1,0:T(8,128)(2,1)}) custom-call(s32[1]{0:T(128)} %bitcast.me, s32[128]{0:T(128)} %partner.13, s32[128]{0:T(128)} %get-tuple-element.13.order, ...), custom_call_target="tpu_custom_call", output_to_operand_aliasing={{2}: (9, {}), {3}: (10, {})} | custom-call | tf_op jit(solution)/shard_map/last/pallas_call | solution.py:509
  (5 shorter events, 0.2 us)
Async XLA Ops:
  8.5 114.0 %all-to-all-start = ((bf16[128,30,8,128]{3,2,1,0:T(8,128)(2,1)}), bf16[128,30,8,128]{3,2,1,0:T(8,128)(2,1)}, u32[]{:S(2)}, u32[]{:S(2)}) async-start(bf16[128,30,8,128]{3,2,1,0:T(8,128)(2,1)} %get-tuple-element.14), calls=%async_computation | async-start | bytes 15728640 | tf_op jit(solution)/shard_map/all_to_all | solution.py:409
  125.4 71.7 %all-to-all-start.1 = ((bf16[128,20,8,128]{3,2,1,0:T(8,128)(2,1)}), bf16[128,20,8,128]{3,2,1,0:T(8,128)(2,1)}, u32[]{:S(2)}, u32[]{:S(2)}) async-start(bf16[128,20,8,128]{3,2,1,0:T(8,128)(2,1)} %second_forward.1), calls=%async_computation.1 | async-start | bytes 10485760 | tf_op jit(solution)/shard_map/all_to_all | solution.py:409
  200.0 9.0 %copy-start = (f32[192]{0:T(256)S(1)}, f32[192]{0:T(256)}, u32[]{:S(2)}) copy-start(f32[192]{0:T(256)} %param.13) | copy-start | bytes 2308
  200.1 9.8 %copy-start.1 = (f32[192]{0:T(256)S(1)}, f32[192]{0:T(256)}, u32[]{:S(2)}) copy-start(f32[192]{0:T(256)} %param.16) | copy-start | bytes 2308
  200.1 112.5 %all-to-all-start.2 = ((bf16[128,30,8,128]{3,2,1,0:T(8,128)(2,1)}), bf16[128,30,8,128]{3,2,1,0:T(8,128)(2,1)}, u32[]{:S(2)}, u32[]{:S(2)}) async-start(bf16[128,30,8,128]{3,2,1,0:T(8,128)(2,1)} %third_forward.1), calls=%async_computation.2 | async-start | bytes 15728640 | tf_op jit(solution)/shard_map/all_to_all | solution.py:409

commit v5 on v4

--- a/solution.py
+++ b/solution.py
@@ -21,6 +21,7 @@
 GROUPS = 8
 SIZE = N // GROUPS
 UNROLL = 4
+FEW = 8
 
 HBM = pl.BlockSpec(memory_space=pltpu.MemorySpace.HBM)
 SMEM = pl.BlockSpec(memory_space=pltpu.SMEM)
@@ -34,34 +35,6 @@
 
 def array_of(t, rows, cols):
     return t.reshape(rows // 8, cols // 128, 8, 128).transpose(0, 2, 1, 3).reshape(1, rows, cols)
-
-
-def copies(partner, visit, after=None):
-    def step(j, counts):
-        movers, stayers = counts
-        p = partner[j]
-        moving = p != j
-        visit(j, moving, jnp.where(moving, movers, stayers), p)
-        one = moving.astype(jnp.int32)
-        return (movers + one, stayers + 1 - one)
-
-    def group(g, counts):
-        counts = lax.fori_loop(g * SIZE, (g + 1) * SIZE, step, counts)
-        if after is not None:
-            after(g)
-        return counts
-
-    lax.fori_loop(0, GROUPS, group, (jnp.int32(0), jnp.int32(0)))
-
-
-def own_piece(w_in, w_out, rank, offset, size, act):
-    @pl.when(rank < 32)
-    def _():
-        act(w_in.at[pl.ds(rank * CHUNK + offset, size)])
-
-    @pl.when(rank >= 32)
-    def _():
-        act(w_out.at[pl.ds((rank - 32) * CHUNK + offset, size)])
 
 
 def go(src, dst, sem, wait):
@@ -70,10 +43,6 @@
         copy.wait()
     else:
         copy.start()
-
-
-def nothing(j, moving, rank, p):
-    pass
 
 
 def column(row):
@@ -205,32 +174,33 @@
         settled(stage.at[:, pl.ds(0, C1)], osem)
 
 
+def in_turn(w_in, w_out, act):
+    half = N // 4
+    for w, start in ((w_in, 0), (w_out, half)):
+        lax.fori_loop(
+            0, half // FEW, lambda g, c: (act(start + g * FEW, w, g * FEW * CHUNK), c)[1], 0
+        )
+
+
 def second_own_kernel(me, partner, order, w_in, w_out, buf2, stage, sem, osem):
     my = me[0]
 
+    def act(first, w, base):
+        for i in range(FEW):
+            tile = base + i * CHUNK
+            go(w.at[pl.ds(tile + C1, C2)], stage.at[i, pl.ds(0, C2)], sem, False)
+            go(w.at[pl.ds(tile + NPART + C1, MA2)], stage.at[i, pl.ds(C2, MA2)], sem, False)
+        settled(stage, sem)
+        for i in range(FEW):
+            m = order[first + i]
+            t = order[first + i + N // 2]
+            go(stage.at[i, pl.ds(0, C2)], buf2.at[t], osem, False)
+            go(stage.at[i, pl.ds(C2, MA2)], buf2.at[m, pl.ds(0, MA2)], osem, False)
+        settled(stage, osem)
+
     @pl.when(partner[my] != my)
     def _():
-        def step(k, w, tile):
-            m = order[k]
-            t = order[k + N // 2]
-            at = sem.at[k // SIZE]
-            go(w.at[pl.ds(tile + C1, C2)], stage.at[k, pl.ds(0, C2)], at, False)
-            go(w.at[pl.ds(tile + NPART + C1, MA2)], stage.at[k, pl.ds(C2, MA2)], at, False)
-
-        both_halves(step, w_in, w_out)
-        for g in range(N // 2 // SIZE):
-            settled(stage.at[group_of(g)], sem.at[g])
-
-            def send(i, c):
-                k = g * SIZE + i
-                m = order[k]
-                t = order[k + N // 2]
-                go(stage.at[k, pl.ds(0, C2)], buf2.at[t], osem, False)
-                go(stage.at[k, pl.ds(C2, MA2)], buf2.at[m, pl.ds(0, MA2)], osem, False)
-                return c
-
-            lax.fori_loop(0, SIZE, send, 0, unroll=UNROLL)
-        settled(stage, osem)
+        in_turn(w_in, w_out, act)
 
 
 def forward_kernel(of_mover, of_stayer, tokens, me, partner, order, recv, *refs):
@@ -250,22 +220,27 @@
     for mine, piece in ((True, of_mover), (False, of_stayer)):
         @pl.when(i_move == mine)
         def _():
-            forward(order, partner, stage, buf, sem, osem, recv, *piece, between)
+            forward(order, partner, stage, buf, sem, osem, recv, *piece, tokens, between)
 
     if tokens:
         go(tok, buf.at[:, pl.ds(C3, TOK)], tsem, True)
 
 
-def forward(order, partner, stage, buf, sem, osem, recv, lo, to, size, between):
+def forward(order, partner, stage, buf, sem, osem, recv, lo, to, size, slow, between):
     groups = N // 2 // SIZE
 
     def load(k):
         p = partner[order[k]]
         go(recv.at[p, pl.ds(lo, size)], stage.at[k, pl.ds(0, size)], sem.at[k // SIZE], False)
 
-    each_mover(load)
-    between()
+    if slow:
+        between()
+    else:
+        each_mover(load)
     for g in range(groups):
+        if slow:
+            for i in range(SIZE):
+                load(g * SIZE + i)
         settled(stage.at[group_of(g), pl.ds(0, size)], sem.at[g])
 
         def send(i, c):
@@ -274,61 +249,48 @@
             return c
 
         lax.fori_loop(0, SIZE, send, 0, unroll=UNROLL)
-    settled(stage.at[pl.ds(0, N // 2), pl.ds(0, size)], osem)
-
-
-def settle_kernel(me, partner, w_in, w_out, recv2, new_in, new_out, stage, sem, osem):
+        if slow:
+            settled(stage.at[group_of(g), pl.ds(0, size)], osem)
+    if not slow:
+        settled(stage.at[pl.ds(0, N // 2), pl.ds(0, size)], osem)
+
+
+def settle_kernel(
+    me, partner, order, w_in, w_out, recv2, new_in, new_out, stage, whole, sem, osem
+):
     my = me[0]
     i_move = partner[my] != my
 
-    def load(wait, g):
-        part = pl.ds(g * SIZE * C2, SIZE * C2)
-        go(recv2.at[part], stage.at[part], sem.at[g], wait)
-
-    def visit(wait, j, moving, rank, p):
-        if not wait:
-            @pl.when(j % SIZE == 0)
-            def _():
-                load(True, j // SIZE)
-
-        @pl.when(moving)
-        def _():
-            own_piece(
-                new_in, new_out, rank, NPART, MB2,
-                lambda dst: go(stage.at[pl.ds(j * C2 + MA2, MB2)], dst, osem, wait),
-            )
-
-        @pl.when(jnp.logical_not(moving))
-        def _():
-            own_piece(
-                new_in, new_out, rank, 0, C2,
-                lambda dst: go(stage.at[pl.ds(j * C2, C2)], dst, osem, wait),
-            )
-
-    @pl.when(i_move)
-    def _():
-        copies(partner, nothing, functools.partial(load, False))
-        copies(partner, functools.partial(visit, False))
-        copies(partner, functools.partial(visit, True))
+    def act(first, w, base):
+        for i in range(FEW):
+            m = order[first + i]
+            t = order[first + i + N // 2]
+            go(recv2.at[t], stage.at[i, pl.ds(0, C2)], sem, False)
+            go(recv2.at[m, pl.ds(MA2, MB2)], stage.at[i, pl.ds(C2, MB2)], sem, False)
+        settled(stage, sem)
+        for i in range(FEW):
+            tile = base + i * CHUNK
+            go(stage.at[i, pl.ds(0, C2)], w.at[pl.ds(tile, C2)], osem, False)
+            go(stage.at[i, pl.ds(C2, MB2)], w.at[pl.ds(tile + NPART, MB2)], osem, False)
+        settled(stage, osem)
+
+    @pl.when(i_move)
+    def _():
+        in_turn(new_in, new_out, act)
 
     @pl.when(jnp.logical_not(i_move))
     def _():
-        size = HALF // GROUPS
-        pieces = [
-            (src.at[pl.ds(g * size, size)], stage.at[pl.ds(h * HALF + g * size, size)],
-             dst.at[pl.ds(g * size, size)], g)
-            for h, (src, dst) in enumerate(((w_in, new_in), (w_out, new_out)))
-            for g in range(GROUPS)
-        ]
-        for h in range(2):
-            half = pieces[h * GROUPS : (h + 1) * GROUPS]
-            for src, mid, dst, g in half:
-                go(src, mid, sem.at[g], False)
-            for src, mid, dst, g in half:
-                go(src, mid, sem.at[g], True)
-                go(mid, dst, osem, False)
-        for src, mid, dst, g in pieces:
-            go(mid, dst, osem, True)
+        size = whole.shape[0]
+        for src, dst in ((w_in, new_in), (w_out, new_out)):
+            def step(g, c):
+                part = pl.ds(g * size, size)
+                go(src.at[part], whole, sem, False)
+                go(src.at[part], whole, sem, True)
+                go(whole, dst.at[part], osem, False)
+                go(whole, dst.at[part], osem, True)
+                return c
+
+            lax.fori_loop(0, HALF // size, step, 0)
 
 
 def last_kernel(
@@ -450,7 +412,7 @@
         out_shape=shape(N, C2, 8, 128),
         in_specs=[SMEM, SMEM, SMEM, HBM, HBM],
         out_specs=HBM,
-        scratch_shapes=[pltpu.VMEM((N // 2, C2 + MA2, 8, 128), BF), SEMS, DMA],
+        scratch_shapes=[pltpu.VMEM((FEW, C2 + MA2, 8, 128), BF), DMA, DMA],
         name="second_own",
     )(me, partner, order, w_in, w_out)
     buf2 = pl.pallas_call(
@@ -501,11 +463,13 @@
     new_in, new_out = pl.pallas_call(
         settle_kernel,
         out_shape=(shape(HALF, 8, 128), shape(HALF, 8, 128)),
-        in_specs=[SMEM, SMEM, HBM, HBM, HBM],
+        in_specs=[SMEM, SMEM, SMEM, HBM, HBM, HBM],
         out_specs=(HBM, HBM),
-        scratch_shapes=[pltpu.VMEM((2 * HALF, 8, 128), BF), SEMS, DMA],
+        scratch_shapes=[
+            pltpu.VMEM((FEW, C2 + MB2, 8, 128), BF), pltpu.VMEM((HALF // 8, 8, 128), BF), DMA, DMA,
+        ],
         name="settle",
-    )(me, partner, w_in, w_out, recv2.reshape(N * C2, 8, 128))
+    )(me, partner, order, w_in, w_out, recv2)
     res_one, res_two, new_in, new_out = pl.pallas_call(
         last_kernel,
         out_shape=(

time: 321 us -> 323 us (level); the launches traced: 320 us -> 318 us
  waiting for transfers between devices: 225 us -> 200 us
  Pallas kernels: 35.6 us -> 57.7 us
    all_to_all x3, waiting for transfers between devices: 225 us -> 200 us  [exchange(): return lax.all_to_all(x, AXES, split_axis=0, concat_axis=0, tiled=True)]
    pallas_call x1, Pallas kernels: 6.47 us -> 30.7 us  [local(): pl.pallas_call(settle_kernel, out_shape=(shape(HALF, 8, 128), shape(HALF,...]
    pallas_call x1, Pallas kernels: 4.38 us -> 8.03 us  [local(): pl.pallas_call(functools.partial(forward_kernel, (MB2, 0, C1 - MB2), (C2,...]
    pallas_call x1, Pallas kernels: 4.07 us -> 0.7 us  [local(): pl.pallas_call(second_own_kernel, out_shape=shape(N, C2, 8, 128), in_spec...]
  transfers between devices with their start and end apart: 3 -> 3, of which waited for: 3 -> 3; matrix products, arithmetic and copies ran while one was open for 10% -> 10% of each run, Pallas kernels for 5% -> 12%
where the time goes in v5:
time: 323 us; the launch traced here: 318 us
  waiting for transfers between devices  200 us (62%)
  Pallas kernels  57.7 us (18%)
  starting transfers between devices  28.2 us (9%)
  matrix products  20.4 us (6%)
  local copies, waits for them, and re-layouts  8.57 us (3%)
    all_to_all x3, waiting for transfers between devices, exchange(): return lax.all_to_all(x, AXES, split_axis=0, concat_axis=0, tiled=True)  200 us
    pallas_call x1, Pallas kernels, local(): pl.pallas_call(settle_kernel, out_shape=(shape(HALF, 8, 128), shape(HALF,...  30.7 us
    all_to_all x3, starting transfers between devices, exchange(): return lax.all_to_all(x, AXES, split_axis=0, concat_axis=0, tiled=True)  28.2 us
    dot_general x1, matrix products, local(): jnp.dot(hidden, weight_out[0], preferred_element_type=jnp.float32)  20.4 us
    pallas_call x1, Pallas kernels, local(): pl.pallas_call(functools.partial(forward_kernel, (MB2, 0, C1 - MB2), (C2,...  8.03 us
  transfers between devices with their start and end apart: 3, of which 3 were waited for; matrix products, arithmetic and copies ran while one was open for 10% of the time, Pallas kernels for 12%

profile of v5, /device:TPU:37, one launch (start us, length us, event | category | flops | bytes accessed | tf_op | source)
XLA Modules:
  0.0 317.5 jit_solution(7500954662658558732)
XLA Ops:
  0.6 6.3 %first.1 = (bf16[128,30,8,128]{3,2,1,0:T(8,128)(2,1)}, s32[384,2]{1,0:T(8,128)}, s32[128]{0:T(128)}) custom-call(s32[1]{0:T(128)} %bitcast.me, s32[128]{0:T(128)} %partner.13, bf16[2304,8,128]{2,1,0:T(8,128)(2,1)} %bitcast.53, bf16[2304,8,128]{2,1,0:T(8,128)(2,1)} %bitcast.56, bf16[192,768]{1,0:T(8,128)(2,1)} %refs_1_.3, bf16[192,768]{1,0:T(8,128)(2,1)} %refs_2_.1, ...), custom_call_target="tpu_custom_call" | custom-call | tf_op jit(solution)/shard_map/first/pallas_call | solution.py:387
  6.9 12.2 %all-to-all-start = ((bf16[128,30,8,128]{3,2,1,0:T(8,128)(2,1)}), bf16[128,30,8,128]{3,2,1,0:T(8,128)(2,1)}, u32[]{:S(2)}, u32[]{:S(2)}) async-start(bf16[128,30,8,128]{3,2,1,0:T(8,128)(2,1)} %get-tuple-element.14), calls=%async_computation | async-start | bytes 15728640 | tf_op jit(solution)/shard_map/all_to_all | solution.py:371
  19.1 0.7 second_own.1.refs_0_
  19.8 102.8 %all-to-all-done.recv = bf16[128,30,8,128]{3,2,1,0:T(8,128)(2,1)} async-done(((bf16[128,30,8,128]{3,2,1,0:T(8,128)(2,1)}), bf16[128,30,8,128]{3,2,1,0:T(8,128)(2,1)}, u32[]{:S(2)}, u32[]{:S(2)}) %all-to-all-start) | async-done | bytes 7864352 | tf_op jit(solution)/shard_map/all_to_all | solution.py:371
  122.6 3.4 %second_forward.1 = bf16[128,20,8,128]{3,2,1,0:T(8,128)(2,1)} custom-call(s32[1]{0:T(128)} %bitcast.me, s32[128]{0:T(128)} %partner.13, s32[128]{0:T(128)} %get-tuple-element.13.order, bf16[128,30,8,128]{3,2,1,0:T(8,128)(2,1)} %all-to-all-done.recv, bf16[128,20,8,128]{3,2,1,0:T(8,128)(2,1)} %second_own.1.refs_0_), custom_call_target="tpu_custom_call", output_to_operand_aliasing={{}: (4, {})} | custom-call | tf_op jit(solution)/shard_map/second_forward/pallas_call | solution.py:418
  126.0 7.6 %all-to-all-start.1 = ((bf16[128,20,8,128]{3,2,1,0:T(8,128)(2,1)}), bf16[128,20,8,128]{3,2,1,0:T(8,128)(2,1)}, u32[]{:S(2)}, u32[]{:S(2)}) async-start(bf16[128,20,8,128]{3,2,1,0:T(8,128)(2,1)} %second_forward.1), calls=%async_computation.1 | async-start | bytes 10485760 | tf_op jit(solution)/shard_map/all_to_all | solution.py:371
  133.6 1.2 slice.20
  134.9 0.6 copy.25
  135.5 0.4 reshape.82
  135.9 1.5 slice_bitcast_fusion.1
  137.4 20.4 %fusion.4 = bf16[1536,768]{1,0:T(8,128)(2,1)} fusion(bf16[1,3072,768]{2,1,0:T(8,128)(2,1)} %param.19, bf16[1,768,3072]{2,1,0:T(8,128)(2,1)} %param.18, bf16[512,768]{1,0:T(8,128)(2,1)S(1)} %reshape.82, bf16[1024,768]{1,0:T(8,128)(2,1)S(1)} %slice_bitcast_fusion.1), kind=kOutput, calls=%fused_computation.4 | convolution fusion | flops 14510850048 | bytes 14155776 | tf_op jit(solution)/shard_map/dot_general | solution.py:437
  157.8 1.2 slice.22
  159.2 0.4 copy.21
  159.6 1.5 slice_bitcast_fusion
  161.1 1.6 pad_maximum_fusion.refs_0_
  162.7 8.0 %third_held.1.refs_0_ = bf16[128,30,8,128]{3,2,1,0:T(8,128)(2,1)} custom-call(s32[1]{0:T(128)} %bitcast.me, s32[128]{0:T(128)} %partner.13, s32[128]{0:T(128)} %get-tuple-element.13.order, bf16[128,30,8,128]{3,2,1,0:T(8,128)(2,1)} %all-to-all-done.recv, bf16[128,9,8,128]{3,2,1,0:T(8,128)(2,1)} %pad_maximum_fusion.refs_0_), custom_call_target="tpu_custom_call" | custom-call | tf_op jit(solution)/shard_map/third_held/pallas_call | solution.py:442
  170.8 26.0 %all-to-all-done.1.recv.recv2 = bf16[128,20,8,128]{3,2,1,0:T(8,128)(2,1)} async-done(((bf16[128,20,8,128]{3,2,1,0:T(8,128)(2,1)}), bf16[128,20,8,128]{3,2,1,0:T(8,128)(2,1)}, u32[]{:S(2)}, u32[]{:S(2)}) %all-to-all-start.1) | async-done | bytes 5242912 | tf_op jit(solution)/shard_map/all_to_all | solution.py:371
  196.7 3.4 %third_forward.1 = bf16[128,30,8,128]{3,2,1,0:T(8,128)(2,1)} custom-call(s32[1]{0:T(128)} %bitcast.me, s32[128]{0:T(128)} %partner.13, s32[128]{0:T(128)} %get-tuple-element.13.order, bf16[128,20,8,128]{3,2,1,0:T(8,128)(2,1)} %all-to-all-done.1.recv.recv2, bf16[128,30,8,128]{3,2,1,0:T(8,128)(2,1)} %third_held.1.refs_0_), custom_call_target="tpu_custom_call", output_to_operand_aliasing={{}: (4, {})} | custom-call | tf_op jit(solution)/shard_map/third_forward/pallas_call | solution.py:453
  200.2 8.5 %all-to-all-start.2 = ((bf16[128,30,8,128]{3,2,1,0:T(8,128)(2,1)}), bf16[128,30,8,128]{3,2,1,0:T(8,128)(2,1)}, u32[]{:S(2)}, u32[]{:S(2)}) async-start(bf16[128,30,8,128]{3,2,1,0:T(8,128)(2,1)} %third_forward.1), calls=%async_computation.2 | async-start | bytes 15728640 | tf_op jit(solution)/shard_map/all_to_all | solution.py:371
  208.7 0.8 copy.22.refs_3_
  209.4 0.8 copy.23.refs_4_
  210.2 30.7 %settle.1 = (bf16[2304,8,128]{2,1,0:T(8,128)(2,1)}, bf16[2304,8,128]{2,1,0:T(8,128)(2,1)}) custom-call(s32[1]{0:T(128)} %bitcast.me, s32[128]{0:T(128)} %partner.13, s32[128]{0:T(128)} %get-tuple-element.13.order, bf16[2304,8,128]{2,1,0:T(8,128)(2,1)} %bitcast.55, bf16[2304,8,128]{2,1,0:T(8,128)(2,1)} %bitcast.58, ...), custom_call_target="tpu_custom_call" | custom-call | tf_op jit(solution)/shard_map/settle/pallas_call | solution.py:463
  240.9 71.3 %all-to-all-done.2.recv3 = bf16[128,30,8,128]{3,2,1,0:T(8,128)(2,1)} async-done(((bf16[128,30,8,128]{3,2,1,0:T(8,128)(2,1)}), bf16[128,30,8,128]{3,2,1,0:T(8,128)(2,1)}, u32[]{:S(2)}, u32[]{:S(2)}) %all-to-all-start.2) | async-done | bytes 7864352 | tf_op jit(solution)/shard_map/all_to_all | solution.py:371
  312.2 5.2 %last.1 = (bf16[192,768]{1,0:T(8,128)(2,1)}, bf16[192,768]{1,0:T(8,128)(2,1)}, bf16[2304,8,128]{2,1,0:T(8,128)(2,1)}, bf16[2304,8,128]{2,1,0:T(8,128)(2,1)}) custom-call(s32[1]{0:T(128)} %bitcast.me, s32[128]{0:T(128)} %partner.13, s32[128]{0:T(128)} %get-tuple-element.13.order, ...), custom_call_target="tpu_custom_call", output_to_operand_aliasing={{2}: (9, {}), {3}: (10, {})} | custom-call | tf_op jit(solution)/shard_map/last/pallas_call | solution.py:473
  (5 shorter events, 0.2 us)
Async XLA Ops:
  6.9 115.7 %all-to-all-start = ((bf16[128,30,8,128]{3,2,1,0:T(8,128)(2,1)}), bf16[128,30,8,128]{3,2,1,0:T(8,128)(2,1)}, u32[]{:S(2)}, u32[]{:S(2)}) async-start(bf16[128,30,8,128]{3,2,1,0:T(8,128)(2,1)} %get-tuple-element.14), calls=%async_computation | async-start | bytes 15728640 | tf_op jit(solution)/shard_map/all_to_all | solution.py:371
  126.0 70.7 %all-to-all-start.1 = ((bf16[128,20,8,128]{3,2,1,0:T(8,128)(2,1)}), bf16[128,20,8,128]{3,2,1,0:T(8,128)(2,1)}, u32[]{:S(2)}, u32[]{:S(2)}) async-start(bf16[128,20,8,128]{3,2,1,0:T(8,128)(2,1)} %second_forward.1), calls=%async_computation.1 | async-start | bytes 10485760 | tf_op jit(solution)/shard_map/all_to_all | solution.py:371
  200.2 8.5 %copy-start = (f32[192]{0:T(256)S(1)}, f32[192]{0:T(256)}, u32[]{:S(2)}) copy-start(f32[192]{0:T(256)} %param.13) | copy-start | bytes 2308
  200.2 9.2 %copy-start.1 = (f32[192]{0:T(256)S(1)}, f32[192]{0:T(256)}, u32[]{:S(2)}) copy-start(f32[192]{0:T(256)} %param.16) | copy-start | bytes 2308
  200.2 112.0 %all-to-all-start.2 = ((bf16[128,30,8,128]{3,2,1,0:T(8,128)(2,1)}), bf16[128,30,8,128]{3,2,1,0:T(8,128)(2,1)}, u32[]{:S(2)}, u32[]{:S(2)}) async-start(bf16[128,30,8,128]{3,2,1,0:T(8,128)(2,1)} %third_forward.1), calls=%async_computation.2 | async-start | bytes 15728640 | tf_op jit(solution)/shard_map/all_to_all | solution.py:371

commit v6 on v3

--- a/solution.py
+++ b/solution.py
@@ -103,11 +103,14 @@
 
 
 def first_kernel(
-    me, partner, w_in, w_out, one, two, routes_one, routes_two, gain, place,
-    buf1, pos, order, stage, sem, osem,
+    me, partner, w_in, w_out, *refs,
 ):
+    given, (buf1, pos_out, order, stage, *held, pos, sem, osem, isem) = refs[:6], refs[6:]
+    one, two, routes_one, routes_two, gain, place = held
     my = me[0]
     i_move = partner[my] != my
+    for src, dst in zip(given, held):
+        go(src, dst, isem, False)
 
     def sort(j, counts):
         movers, stayers = counts
@@ -132,6 +135,8 @@
     width = one.shape[1]
     cols = width // 128
     total = 2 * rows
+    for src, dst in zip(given, held):
+        go(src, dst, isem, True)
     slots = place[...]
     lower = (
         lax.broadcasted_iota(jnp.int32, (rows, rows), 1)
@@ -158,6 +163,7 @@
     late = jnp.where(place_in < 8, -1, target * 8 + place_in - 8)
     pos[:, 0:1] = early
     pos[:, 1:2] = late
+    go(pos, pos_out, isem, False)
 
     def tiles(lo, size):
         go(stage.at[:, pl.ds(lo, size)], buf1.at[:, pl.ds(lo, size)], osem, False)
@@ -191,6 +197,7 @@
     for c in range(cols):
         stage[:, C1 + c] = cut(top, c).astype(BF)
     tiles(C1, cols)
+    go(pos, pos_out, isem, True)
     settled(stage.at[:, pl.ds(C1, TOK)], osem)
 
     @pl.when(i_move)
@@ -327,9 +334,11 @@
 
 
 def last_kernel(
-    me, partner, order, recv3, pos, one, two, gate_one, gate_two, in_, out_,
-    res_one, res_two, new_in, new_out, stage, tok, sem, osem, tsem,
+    me, partner, order, recv3, *refs,
 ):
+    given, (in_, out_, *results, new_in, new_out) = refs[:5], refs[5:11]
+    stage, tok, *held, res_one, res_two, sem, osem, tsem, isem = refs[11:]
+    pos, one, two, gate_one, gate_two = held
     my = me[0]
     i_move = partner[my] != my
     go(recv3.at[:, pl.ds(C3, TOK)], tok, tsem, False)
@@ -343,10 +352,14 @@
         for g in range(GROUPS):
             load(False, g)
 
+    for src, dst in zip(given, held):
+        go(src, dst, isem, False)
     rows = one.shape[0]
     width = one.shape[1]
     cols = width // 128
     total = 2 * rows
+    for src, dst in zip(given, held):
+        go(src, dst, isem, True)
     early = pos[:, 0:1]
     late = pos[:, 1:2]
     lane = lax.broadcasted_iota(jnp.int32, (total, N * 8), 1)
@@ -381,6 +394,9 @@
             h = slice(c // 2 * 128, (c // 2 + 1) * 128)
             answer = top[r, s] + (odd if c % 2 else even)[r, h]
             res[:, s] = (group[:, s].astype(jnp.float32) + gate[...] * answer).astype(BF)
+        go(res, results[b], isem, False)
+    for b, res in enumerate((res_one, res_two)):
+        go(res, results[b], isem, True)
 
     @pl.when(i_move)
     def _():
@@ -415,9 +431,15 @@
             shape(2 * rows, 2, dtype=jnp.int32),
             shape(N, dtype=jnp.int32),
         ),
-        in_specs=[SMEM, SMEM, HBM, HBM] + [VMEM] * 6,
-        out_specs=(HBM, VMEM, SMEM),
-        scratch_shapes=[pltpu.VMEM((N, C1 + TOK, 8, 128), BF), SEMS, DMA],
+        in_specs=[SMEM, SMEM, HBM, HBM] + [HBM] * 6,
+        out_specs=(HBM, HBM, SMEM),
+        scratch_shapes=[
+            pltpu.VMEM((N, C1 + TOK, 8, 128), BF),
+            pltpu.VMEM((rows, width), BF), pltpu.VMEM((rows, width), BF),
+            pltpu.VMEM((1, rows), jnp.int32), pltpu.VMEM((1, rows), jnp.int32),
+            pltpu.VMEM((width // 128, 128), jnp.float32), pltpu.VMEM((1, N), jnp.int32),
+            pltpu.VMEM((2 * rows, 2), jnp.int32), SEMS, DMA, DMA,
+        ],
         name="first",
     )(
         me, partner, w_in, w_out, group_one, group_two,
@@ -472,10 +494,15 @@
         out_shape=(
             shape(rows, width), shape(rows, width), shape(HALF, 8, 128), shape(HALF, 8, 128),
         ),
-        in_specs=[SMEM, SMEM, SMEM, HBM] + [VMEM] * 5 + [HBM, HBM],
-        out_specs=(VMEM, VMEM, HBM, HBM),
+        in_specs=[SMEM, SMEM, SMEM, HBM] + [HBM] * 7,
+        out_specs=(HBM, HBM, HBM, HBM),
         scratch_shapes=[
-            pltpu.VMEM((N, C3, 8, 128), BF), pltpu.VMEM((N, TOK, 8, 128), BF), SEMS, DMA, DMA,
+            pltpu.VMEM((N, C3, 8, 128), BF), pltpu.VMEM((N, TOK, 8, 128), BF),
+            pltpu.VMEM((2 * rows, 2), jnp.int32),
+            pltpu.VMEM((rows, width), BF), pltpu.VMEM((rows, width), BF),
+            pltpu.VMEM((rows, 1), jnp.float32), pltpu.VMEM((rows, 1), jnp.float32),
+            pltpu.VMEM((rows, width), BF), pltpu.VMEM((rows, width), BF),
+            SEMS, DMA, DMA, DMA,
         ],
         input_output_aliases={9: 2, 10: 3},
         name="last",

time: 316 us -> 316 us (level)
  Pallas kernels: 28.1 us -> 31.5 us
  transfers between devices with their start and end apart: 2 -> 2, of which waited for: 2 -> 2; matrix products, arithmetic and copies ran while one was open for 9% -> 9% of each run, Pallas kernels for 3% -> 2%
where the time goes in v6:
time: 316 us; the launch traced here: 314 us
  waiting for transfers between devices  131 us (41%)
  blocking collectives  105 us (33%)
  Pallas kernels  31.5 us (10%)
  matrix products  20.4 us (6%)
  starting transfers between devices  16.5 us (5%)
  local copies, waits for them, and re-layouts  7.36 us (2%)
    all_to_all x2, waiting for transfers between devices, exchange(): return lax.all_to_all(x, AXES, split_axis=0, concat_axis=0, tiled=True)  131 us
    all_to_all x1, blocking collectives, exchange(): return lax.all_to_all(x, AXES, split_axis=0, concat_axis=0, tiled=True)  105 us
    dot_general x1, matrix products, local(): jnp.dot(hidden, weight_out[0], preferred_element_type=jnp.float32)  20.4 us
    all_to_all x2, starting transfers between devices, exchange(): return lax.all_to_all(x, AXES, split_axis=0, concat_axis=0, tiled=True)  16.5 us
    pallas_call x1, Pallas kernels, local(): pl.pallas_call(first_kernel, out_shape=(shape(N, C1 + TOK, 8, 128), shape...  7.85 us
    pallas_call x1, Pallas kernels, local(): pl.pallas_call(last_kernel, out_shape=(shape(rows, width), shape(rows, wi...  7.02 us
    pallas_call x1, Pallas kernels, local(): pl.pallas_call(settle_kernel, out_shape=(shape(HALF, 8, 128), shape(HALF,...  6.47 us
  transfers between devices with their start and end apart: 2, of which 2 were waited for; matrix products, arithmetic and copies ran while one was open for 9% of the time, Pallas kernels for 2%

profile of v6, /device:TPU:37, one launch (start us, length us, event | category | flops | bytes accessed | tf_op | source)
XLA Modules:
  0.0 314.5 jit_solution(9358818918912854289)
XLA Ops:
  0.6 7.8 %first.1 = (bf16[128,30,8,128]{3,2,1,0:T(8,128)(2,1)}, s32[384,2]{1,0:T(8,128)}, s32[128]{0:T(128)}) custom-call(s32[1]{0:T(128)} %bitcast.me, s32[128]{0:T(128)} %partner.9, bf16[2304,8,128]{2,1,0:T(8,128)(2,1)} %bitcast.55, bf16[2304,8,128]{2,1,0:T(8,128)(2,1)} %bitcast.58, bf16[192,768]{1,0:T(8,128)(2,1)} %refs_1_.3, bf16[192,768]{1,0:T(8,128)(2,1)} %refs_2_.1, ...), custom_call_target="tpu_custom_call" | custom-call | tf_op jit(solution)/shard_map/first/pallas_call | solution.py:427
  8.5 105.3 %all_to_all.15.recv1 = bf16[128,30,8,128]{3,2,1,0:T(8,128)(2,1)} all-to-all(bf16[128,30,8,128]{3,2,1,0:T(8,128)(2,1)} %get-tuple-element.14), channel_id=1, replica_groups=mesh['gx'=8,'gy'=16] {'gx','gy'}, dimensions={0} | all-to-all | bytes 15728640 | tf_op jit(solution)/shard_map/all_to_all | solution.py:411
  113.8 5.4 %second.1 = bf16[128,20,8,128]{3,2,1,0:T(8,128)(2,1)} custom-call(s32[1]{0:T(128)} %bitcast.me, s32[128]{0:T(128)} %partner.9, s32[128]{0:T(128)} %get-tuple-element.13.order, bf16[2304,8,128]{2,1,0:T(8,128)(2,1)} %bitcast.56, bf16[2304,8,128]{2,1,0:T(8,128)(2,1)} %bitcast.59, bf16[128,30,8,128]{3,2,1,0:T(8,128)(2,1)} %all_to_all.15.recv1), custom_call_target="tpu_custom_call" | custom-call | tf_op jit(solution)/shard_map/second/pallas_call | solution.py:450
  119.3 0.0 slice-start
  119.3 8.1 %all-to-all-start.1 = ((bf16[128,20,8,128]{3,2,1,0:T(8,128)(2,1)}), bf16[128,20,8,128]{3,2,1,0:T(8,128)(2,1)}, u32[]{:S(2)}, u32[]{:S(2)}) async-start(bf16[128,20,8,128]{3,2,1,0:T(8,128)(2,1)} %second.1), calls=%async_computation.1 | async-start | bytes 10485760 | tf_op jit(solution)/shard_map/all_to_all | solution.py:411
  127.4 0.6 copy.23
  128.0 0.4 reshape.85
  128.4 1.5 slice_bitcast_fusion.1
  129.9 20.4 %fusion.4 = bf16[1536,768]{1,0:T(8,128)(2,1)} fusion(bf16[1,3072,768]{2,1,0:T(8,128)(2,1)} %param.19, bf16[1,768,3072]{2,1,0:T(8,128)(2,1)} %param.18, bf16[512,768]{1,0:T(8,128)(2,1)S(1)} %reshape.85, bf16[1024,768]{1,0:T(8,128)(2,1)S(1)} %slice_bitcast_fusion.1), kind=kOutput, calls=%fused_computation.4 | convolution fusion | flops 14510850048 | bytes 14155776 | tf_op jit(solution)/shard_map/dot_general | solution.py:468
  150.4 1.2 slice.22
  151.6 0.2 reshape.87
  151.8 0.4 copy.19
  152.2 1.5 slice_bitcast_fusion
  153.7 1.6 pad_maximum_fusion.answers
  155.3 35.3 %all-to-all-done.1.recv2 = bf16[128,20,8,128]{3,2,1,0:T(8,128)(2,1)} async-done(((bf16[128,20,8,128]{3,2,1,0:T(8,128)(2,1)}), bf16[128,20,8,128]{3,2,1,0:T(8,128)(2,1)}, u32[]{:S(2)}, u32[]{:S(2)}) %all-to-all-start.1) | async-done | bytes 5242912 | tf_op jit(solution)/shard_map/all_to_all | solution.py:411
  190.6 4.8 %third.1 = bf16[128,30,8,128]{3,2,1,0:T(8,128)(2,1)} custom-call(s32[1]{0:T(128)} %bitcast.me, s32[128]{0:T(128)} %partner.9, s32[128]{0:T(128)} %get-tuple-element.13.order, bf16[128,30,8,128]{3,2,1,0:T(8,128)(2,1)} %all_to_all.15.recv1, bf16[128,20,8,128]{3,2,1,0:T(8,128)(2,1)} %all-to-all-done.1.recv2, bf16[128,9,8,128]{3,2,1,0:T(8,128)(2,1)} %pad_maximum_fusion.answers), custom_call_target="tpu_custom_call" | custom-call | tf_op jit(solution)/shard_map/third/pallas_call | solution.py:473
  195.3 0.0 copy-start
  195.3 0.0 copy-start.1
  195.3 8.4 %all-to-all-start.2 = ((bf16[128,30,8,128]{3,2,1,0:T(8,128)(2,1)}), bf16[128,30,8,128]{3,2,1,0:T(8,128)(2,1)}, u32[]{:S(2)}, u32[]{:S(2)}) async-start(bf16[128,30,8,128]{3,2,1,0:T(8,128)(2,1)} %third.1), calls=%async_computation.2 | async-start | bytes 15728640 | tf_op jit(solution)/shard_map/all_to_all | solution.py:411
  203.8 0.8 copy.20.refs_3_
  204.5 0.8 copy.21.refs_4_
  205.3 6.5 %settle.1 = (bf16[2304,8,128]{2,1,0:T(8,128)(2,1)}, bf16[2304,8,128]{2,1,0:T(8,128)(2,1)}) custom-call(s32[1]{0:T(128)} %bitcast.me, s32[128]{0:T(128)} %partner.9, bf16[2304,8,128]{2,1,0:T(8,128)(2,1)} %bitcast.57, bf16[2304,8,128]{2,1,0:T(8,128)(2,1)} %bitcast.60, bf16[2560,8,128]{2,1,0:T(8,128)(2,1)} %bitcast.27.recv2), custom_call_target="tpu_custom_call" | custom-call | tf_op jit(solution)/shard_map/settle/pallas_call | solution.py:484
  211.8 95.5 %all-to-all-done.2.recv3 = bf16[128,30,8,128]{3,2,1,0:T(8,128)(2,1)} async-done(((bf16[128,30,8,128]{3,2,1,0:T(8,128)(2,1)}), bf16[128,30,8,128]{3,2,1,0:T(8,128)(2,1)}, u32[]{:S(2)}, u32[]{:S(2)}) %all-to-all-start.2) | async-done | bytes 7864352 | tf_op jit(solution)/shard_map/all_to_all | solution.py:411
  307.3 7.0 %last.1 = (bf16[192,768]{1,0:T(8,128)(2,1)}, bf16[192,768]{1,0:T(8,128)(2,1)}, bf16[2304,8,128]{2,1,0:T(8,128)(2,1)}, bf16[2304,8,128]{2,1,0:T(8,128)(2,1)}) custom-call(s32[1]{0:T(128)} %bitcast.me, s32[128]{0:T(128)} %partner.9, s32[128]{0:T(128)} %get-tuple-element.13.order, ...), custom_call_target="tpu_custom_call", output_to_operand_aliasing={{2}: (9, {}), {3}: (10, {})} | custom-call | tf_op jit(solution)/shard_map/last/pallas_call | solution.py:492
  (3 shorter events, 0.0 us)
Async XLA Ops:
  119.3 8.1 %slice-start = ((bf16[128,30,8,128]{3,2,1,0:T(8,128)(2,1)}), bf16[128,3,8,128]{3,2,1,0:T(8,128)(2,1)S(1)}, s32[]{:S(2)}) async-start(bf16[128,30,8,128]{3,2,1,0:T(8,128)(2,1)} %all_to_all.15.recv1), calls=%async_computation.3 | async-start | bytes 1572864 | tf_op jit(solution)/shard_map/slice | solution.py:462
  119.3 71.3 %all-to-all-start.1 = ((bf16[128,20,8,128]{3,2,1,0:T(8,128)(2,1)}), bf16[128,20,8,128]{3,2,1,0:T(8,128)(2,1)}, u32[]{:S(2)}, u32[]{:S(2)}) async-start(bf16[128,20,8,128]{3,2,1,0:T(8,128)(2,1)} %second.1), calls=%async_computation.1 | async-start | bytes 10485760 | tf_op jit(solution)/shard_map/all_to_all | solution.py:411
  195.3 8.4 %copy-start = (f32[192]{0:T(256)S(1)}, f32[192]{0:T(256)}, u32[]{:S(2)}) copy-start(f32[192]{0:T(256)} %param.13) | copy-start | bytes 2308
  195.3 9.2 %copy-start.1 = (f32[192]{0:T(256)S(1)}, f32[192]{0:T(256)}, u32[]{:S(2)}) copy-start(f32[192]{0:T(256)} %param.16) | copy-start | bytes 2308
  195.3 111.9 %all-to-all-start.2 = ((bf16[128,30,8,128]{3,2,1,0:T(8,128)(2,1)}), bf16[128,30,8,128]{3,2,1,0:T(8,128)(2,1)}, u32[]{:S(2)}, u32[]{:S(2)}) async-start(bf16[128,30,8,128]{3,2,1,0:T(8,128)(2,1)} %third.1), calls=%async_computation.2 | async-start | bytes 15728640 | tf_op jit(solution)/shard_map/all_to_all | solution.py:411

commit v7 on v6

--- a/solution.py
+++ b/solution.py
@@ -18,7 +18,7 @@
 NPART = 41
 MA2 = 10
 MB2 = C2 - MA2
-GROUPS = 8
+GROUPS = 4
 SIZE = N // GROUPS
 UNROLL = 4
 

time: 316 us -> 316 us (level)
  no operation moved by 1% of the time
where the time goes in v7:
time: 316 us; the launch traced here: 315 us
  waiting for transfers between devices  131 us (41%)
  blocking collectives  106 us (34%)
  Pallas kernels  30.9 us (10%)
  matrix products  20.5 us (6%)
  starting transfers between devices  17.5 us (6%)
  local copies, waits for them, and re-layouts  7.36 us (2%)
    all_to_all x2, waiting for transfers between devices, exchange(): return lax.all_to_all(x, AXES, split_axis=0, concat_axis=0, tiled=True)  131 us
    all_to_all x1, blocking collectives, exchange(): return lax.all_to_all(x, AXES, split_axis=0, concat_axis=0, tiled=True)  106 us
    dot_general x1, matrix products, local(): jnp.dot(hidden, weight_out[0], preferred_element_type=jnp.float32)  20.5 us
    all_to_all x2, starting transfers between devices, exchange(): return lax.all_to_all(x, AXES, split_axis=0, concat_axis=0, tiled=True)  17.5 us
    pallas_call x1, Pallas kernels, local(): pl.pallas_call(first_kernel, out_shape=(shape(N, C1 + TOK, 8, 128), shape...  7.81 us
    pallas_call x1, Pallas kernels, local(): pl.pallas_call(last_kernel, out_shape=(shape(rows, width), shape(rows, wi...  7.02 us
    pallas_call x1, Pallas kernels, local(): pl.pallas_call(settle_kernel, out_shape=(shape(HALF, 8, 128), shape(HALF,...  6.57 us
  transfers between devices with their start and end apart: 2, of which 2 were waited for; matrix products, arithmetic and copies ran while one was open for 9% of the time, Pallas kernels for 2%

profile of v7, /device:TPU:37, one launch (start us, length us, event | category | flops | bytes accessed | tf_op | source)
XLA Modules:
  0.0 315.0 jit_solution(4244479543402644577)
XLA Ops:
  0.6 7.8 %first.1 = (bf16[128,30,8,128]{3,2,1,0:T(8,128)(2,1)}, s32[384,2]{1,0:T(8,128)}, s32[128]{0:T(128)}) custom-call(s32[1]{0:T(128)} %bitcast.me, s32[128]{0:T(128)} %partner.9, bf16[2304,8,128]{2,1,0:T(8,128)(2,1)} %bitcast.55, bf16[2304,8,128]{2,1,0:T(8,128)(2,1)} %bitcast.58, bf16[192,768]{1,0:T(8,128)(2,1)} %refs_1_.3, bf16[192,768]{1,0:T(8,128)(2,1)} %refs_2_.1, ...), custom_call_target="tpu_custom_call" | custom-call | tf_op jit(solution)/shard_map/first/pallas_call | solution.py:427
  8.5 105.6 %all_to_all.15.recv1 = bf16[128,30,8,128]{3,2,1,0:T(8,128)(2,1)} all-to-all(bf16[128,30,8,128]{3,2,1,0:T(8,128)(2,1)} %get-tuple-element.14), channel_id=1, replica_groups=mesh['gx'=8,'gy'=16] {'gx','gy'}, dimensions={0} | all-to-all | bytes 15728640 | tf_op jit(solution)/shard_map/all_to_all | solution.py:411
  114.1 4.8 %second.1 = bf16[128,20,8,128]{3,2,1,0:T(8,128)(2,1)} custom-call(s32[1]{0:T(128)} %bitcast.me, s32[128]{0:T(128)} %partner.9, s32[128]{0:T(128)} %get-tuple-element.13.order, bf16[2304,8,128]{2,1,0:T(8,128)(2,1)} %bitcast.56, bf16[2304,8,128]{2,1,0:T(8,128)(2,1)} %bitcast.59, bf16[128,30,8,128]{3,2,1,0:T(8,128)(2,1)} %all_to_all.15.recv1), custom_call_target="tpu_custom_call" | custom-call | tf_op jit(solution)/shard_map/second/pallas_call | solution.py:450
  118.8 0.0 slice-start
  118.8 9.0 %all-to-all-start.1 = ((bf16[128,20,8,128]{3,2,1,0:T(8,128)(2,1)}), bf16[128,20,8,128]{3,2,1,0:T(8,128)(2,1)}, u32[]{:S(2)}, u32[]{:S(2)}) async-start(bf16[128,20,8,128]{3,2,1,0:T(8,128)(2,1)} %second.1), calls=%async_computation.1 | async-start | bytes 10485760 | tf_op jit(solution)/shard_map/all_to_all | solution.py:411
  127.9 0.6 copy.23
  128.5 0.4 reshape.85
  128.9 1.5 slice_bitcast_fusion.1
  130.4 20.5 %fusion.4 = bf16[1536,768]{1,0:T(8,128)(2,1)} fusion(bf16[1,3072,768]{2,1,0:T(8,128)(2,1)} %param.19, bf16[1,768,3072]{2,1,0:T(8,128)(2,1)} %param.18, bf16[512,768]{1,0:T(8,128)(2,1)S(1)} %reshape.85, bf16[1024,768]{1,0:T(8,128)(2,1)S(1)} %slice_bitcast_fusion.1), kind=kOutput, calls=%fused_computation.4 | convolution fusion | flops 14510850048 | bytes 14155776 | tf_op jit(solution)/shard_map/dot_general | solution.py:468
  150.9 1.2 slice.22
  152.0 0.2 reshape.87
  152.2 0.4 copy.19
  152.6 1.5 slice_bitcast_fusion
  154.2 1.6 pad_maximum_fusion.answers
  155.8 35.2 %all-to-all-done.1.recv2 = bf16[128,20,8,128]{3,2,1,0:T(8,128)(2,1)} async-done(((bf16[128,20,8,128]{3,2,1,0:T(8,128)(2,1)}), bf16[128,20,8,128]{3,2,1,0:T(8,128)(2,1)}, u32[]{:S(2)}, u32[]{:S(2)}) %all-to-all-start.1) | async-done | bytes 5242912 | tf_op jit(solution)/shard_map/all_to_all | solution.py:411
  191.0 4.8 %third.1 = bf16[128,30,8,128]{3,2,1,0:T(8,128)(2,1)} custom-call(s32[1]{0:T(128)} %bitcast.me, s32[128]{0:T(128)} %partner.9, s32[128]{0:T(128)} %get-tuple-element.13.order, bf16[128,30,8,128]{3,2,1,0:T(8,128)(2,1)} %all_to_all.15.recv1, bf16[128,20,8,128]{3,2,1,0:T(8,128)(2,1)} %all-to-all-done.1.recv2, bf16[128,9,8,128]{3,2,1,0:T(8,128)(2,1)} %pad_maximum_fusion.answers), custom_call_target="tpu_custom_call" | custom-call | tf_op jit(solution)/shard_map/third/pallas_call | solution.py:473
  195.7 0.0 copy-start
  195.8 0.0 copy-start.1
  195.8 8.5 %all-to-all-start.2 = ((bf16[128,30,8,128]{3,2,1,0:T(8,128)(2,1)}), bf16[128,30,8,128]{3,2,1,0:T(8,128)(2,1)}, u32[]{:S(2)}, u32[]{:S(2)}) async-start(bf16[128,30,8,128]{3,2,1,0:T(8,128)(2,1)} %third.1), calls=%async_computation.2 | async-start | bytes 15728640 | tf_op jit(solution)/shard_map/all_to_all | solution.py:411
  204.2 0.8 copy.20.refs_3_
  205.0 0.8 copy.21.refs_4_
  205.8 6.6 %settle.1 = (bf16[2304,8,128]{2,1,0:T(8,128)(2,1)}, bf16[2304,8,128]{2,1,0:T(8,128)(2,1)}) custom-call(s32[1]{0:T(128)} %bitcast.me, s32[128]{0:T(128)} %partner.9, bf16[2304,8,128]{2,1,0:T(8,128)(2,1)} %bitcast.57, bf16[2304,8,128]{2,1,0:T(8,128)(2,1)} %bitcast.60, bf16[2560,8,128]{2,1,0:T(8,128)(2,1)} %bitcast.27.recv2), custom_call_target="tpu_custom_call" | custom-call | tf_op jit(solution)/shard_map/settle/pallas_call | solution.py:484
  212.4 95.4 %all-to-all-done.2.recv3 = bf16[128,30,8,128]{3,2,1,0:T(8,128)(2,1)} async-done(((bf16[128,30,8,128]{3,2,1,0:T(8,128)(2,1)}), bf16[128,30,8,128]{3,2,1,0:T(8,128)(2,1)}, u32[]{:S(2)}, u32[]{:S(2)}) %all-to-all-start.2) | async-done | bytes 7864352 | tf_op jit(solution)/shard_map/all_to_all | solution.py:411
  307.8 7.0 %last.1 = (bf16[192,768]{1,0:T(8,128)(2,1)}, bf16[192,768]{1,0:T(8,128)(2,1)}, bf16[2304,8,128]{2,1,0:T(8,128)(2,1)}, bf16[2304,8,128]{2,1,0:T(8,128)(2,1)}) custom-call(s32[1]{0:T(128)} %bitcast.me, s32[128]{0:T(128)} %partner.9, s32[128]{0:T(128)} %get-tuple-element.13.order, ...), custom_call_target="tpu_custom_call", output_to_operand_aliasing={{2}: (9, {}), {3}: (10, {})} | custom-call | tf_op jit(solution)/shard_map/last/pallas_call | solution.py:492
  (3 shorter events, 0.0 us)
Async XLA Ops:
  118.8 9.0 %slice-start = ((bf16[128,30,8,128]{3,2,1,0:T(8,128)(2,1)}), bf16[128,3,8,128]{3,2,1,0:T(8,128)(2,1)S(1)}, s32[]{:S(2)}) async-start(bf16[128,30,8,128]{3,2,1,0:T(8,128)(2,1)} %all_to_all.15.recv1), calls=%async_computation.3 | async-start | bytes 1572864 | tf_op jit(solution)/shard_map/slice | solution.py:462
  118.8 72.2 %all-to-all-start.1 = ((bf16[128,20,8,128]{3,2,1,0:T(8,128)(2,1)}), bf16[128,20,8,128]{3,2,1,0:T(8,128)(2,1)}, u32[]{:S(2)}, u32[]{:S(2)}) async-start(bf16[128,20,8,128]{3,2,1,0:T(8,128)(2,1)} %second.1), calls=%async_computation.1 | async-start | bytes 10485760 | tf_op jit(solution)/shard_map/all_to_all | solution.py:411
  195.7 8.5 %copy-start = (f32[192]{0:T(256)S(1)}, f32[192]{0:T(256)}, u32[]{:S(2)}) copy-start(f32[192]{0:T(256)} %param.13) | copy-start | bytes 2308
  195.8 9.3 %copy-start.1 = (f32[192]{0:T(256)S(1)}, f32[192]{0:T(256)}, u32[]{:S(2)}) copy-start(f32[192]{0:T(256)} %param.16) | copy-start | bytes 2308
  195.8 112.0 %all-to-all-start.2 = ((bf16[128,30,8,128]{3,2,1,0:T(8,128)(2,1)}), bf16[128,30,8,128]{3,2,1,0:T(8,128)(2,1)}, u32[]{:S(2)}, u32[]{:S(2)}) async-start(bf16[128,30,8,128]{3,2,1,0:T(8,128)(2,1)} %third.1), calls=%async_computation.2 | async-start | bytes 15728640 | tf_op jit(solution)/shard_map/all_to_all | solution.py:411
